TPU v7x, 512 devices: a whole 4x8x8 slice. The times are simulated.
512 devices in a mesh: dp: 16 (over x, z_hi), pack: 32 (over z_lo, y, core).
Axes of the slice: x: 4, y: 8, z: 8 (z_hi: 4, z_lo: 2; z = z_hi * 2 + z_lo), core: 2. Of those that a mesh axis runs over, the one named last changes fastest.
Arguments:
- hidden_in: bfloat16 [1024, 4096], P('dp', 'pack'), may hold values from -6 to 6
- attn_gain: float32 [4096], P('pack'), may hold values from 0.25 to 1.75
- w_query: bfloat16 [4096, 4096], P(None, 'pack'), may hold values from -0.09375 to 0.09375
- query_gain: float32 [128], replicated, may hold values from 0.25 to 1.75
- cached_keys: bfloat16 [163840, 1024], P(('dp', 'pack')), may hold values from -200 to 200
- cached_values: bfloat16 [163840, 1024], P(('dp', 'pack')), may hold values from -9 to 9
- w_out: bfloat16 [4096, 4096], P('pack'), may hold values from -0.09375 to 0.09375
- final_gain: float32 [4096], P('pack'), may hold values from 0.25 to 1.75
- lengths: int32 [16, 64], P('dp'), may hold values from 16 to 304, as said below
- pack_order: int32 [16, 64], P('dp'), may hold values from 0 to 63, each once within a row
- partner: int32 [1024], replicated, may hold values from 0 to 1023, as said below
Outputs:
- pooled: bfloat16 [1024, 4096], P('dp', 'pack')
- loss_rows: float32 [1024], P(('dp', 'pack'))
- grad_hidden: bfloat16 [1024, 4096], P('dp', 'pack')
Inputs may be any that keep to these rules, and one draw needn't show every extreme that they name: Statements 2k and 2k+1 of a group have lengths that sum to 320, so a group's lengths sum to 320 * 32. `pack_order`: each row is a permutation of the group's statement indices. `partner`: no statement is its own positive.
All inputs are finite; a program needn't handle non-finite values.
Results may differ from a plain program's by a relative error of at most 0.019.
Values may be sent and summed in bfloat16 or wider, within the bound.
A program may use at most 128 MiB of HBM per device.

v0:
```python
import jax
import jax.numpy as jnp
from jax import lax
from jax.sharding import PartitionSpec as P

EPSILON = 1e-06
SOFTMAX_WARMTH = 0.05
ROPE_BASE = 1000000.0
MASKED_LOGIT = -1e30


def from_everyone(array, axis):
    copies = jnp.broadcast_to(array, (lax.axis_size(axis), *array.shape))
    return lax.all_to_all(copies, axis, split_axis=0, concat_axis=0, tiled=True)


def over_copies(array, axis):
    return from_everyone(array, axis).sum(axis=0)


def in_order(tiles, dim):
    tiles = jnp.moveaxis(tiles, 0, dim)
    lengths = tiles.shape
    return tiles.reshape(*lengths[:dim], lengths[dim] * lengths[dim + 1], *lengths[dim + 2 :])


def collect(array, axis, dim):
    tiles = from_everyone(array, axis)
    return in_order(tiles, dim)


def in_blocks(array, dim, devices):
    before, after = (array.shape[:dim], array.shape[dim + 1 :])
    return jnp.moveaxis(array.reshape(*before, devices, -1, *after), dim, 0)


def sent_and_summed(array, axis, dim):
    tiles = in_blocks(array, dim, lax.axis_size(axis))
    arrived = lax.all_to_all(tiles, axis, split_axis=0, concat_axis=0, tiled=True)
    return arrived.astype(jnp.float32).sum(axis=0)


def rows_for(lines, devices):
    spare = -len(lines) % devices
    return jnp.pad(lines, [(0, spare)] + [(0, 0)] * (lines.ndim - 1))


def total_of(array, axes):
    lines = array.reshape(-1, array.shape[-1])
    own = sent_and_summed(rows_for(lines, lax.axis_size(axes)), axes, 0)
    whole = collect(own.astype(jnp.bfloat16), axes, 0)
    return whole[: len(lines)].reshape(array.shape).astype(jnp.float32)


def rotate_heads(queries, position):
    head_dim = queries.shape[-1]
    half_dim = head_dim // 2
    frequency = jnp.power(
        jnp.float32(ROPE_BASE), -jnp.arange(half_dim).astype(jnp.float32) * 2.0 / head_dim
    )
    angles = position[:, None] * frequency[None, :]
    cosine = jnp.concatenate([jnp.cos(angles), jnp.cos(angles)], axis=1)[:, None, :]
    sine_part = jnp.concatenate([jnp.sin(angles), jnp.sin(angles)], axis=1)[:, None, :]
    turned = jnp.concatenate([-queries[..., half_dim:], queries[..., :half_dim]], axis=-1)
    return queries * cosine + turned * sine_part


def token_owner(lengths_row, order_row, first_token, token_count):
    stmt_count = order_row.shape[0]
    picked = order_row[:, None] == jnp.arange(stmt_count, dtype=jnp.int32)[None, :]
    packed_len = jnp.sum(jnp.where(picked, lengths_row[None, :], 0), axis=1)
    range_end = jnp.cumsum(packed_len)
    token_index = first_token + jnp.arange(token_count, dtype=jnp.int32)
    slot_index = jnp.sum((token_index[:, None] >= range_end[None, :]).astype(jnp.int32), axis=1)
    return jnp.take(order_row, slot_index)


def block_attention(all_queries, cached_keys, cached_values, token_owners, score_scale):
    stmt_count, head_count, head_dim = all_queries.shape
    kv_heads = cached_keys.shape[1] // head_dim
    group_size = head_count // kv_heads
    grouped = all_queries.reshape(stmt_count, kv_heads, group_size, head_dim)
    key_heads = cached_keys.reshape(-1, kv_heads, head_dim)
    value_heads = cached_values.reshape(-1, kv_heads, head_dim)
    scores = (
        jnp.einsum("skgd,tkd->skgt", grouped, key_heads, preferred_element_type=jnp.float32)
        * score_scale
    )
    token_mask = (token_owners[None, :] == jnp.arange(stmt_count, dtype=jnp.int32)[:, None])[
        :, None, None, :
    ]
    block_max = jnp.max(jnp.where(token_mask, scores, MASKED_LOGIT), axis=3)
    softmax_weights = jnp.where(token_mask, jnp.exp(scores - block_max[..., None]), 0.0)
    block_sum = jnp.sum(softmax_weights, axis=3)
    numerators = jnp.einsum(
        "skgt,tkd->skgd",
        softmax_weights.astype(jnp.bfloat16),
        value_heads,
        preferred_element_type=jnp.float32,
    )
    return (
        block_max.reshape(stmt_count, head_count),
        block_sum.reshape(stmt_count, head_count),
        numerators.reshape(stmt_count, head_count, head_dim),
    )


def masked_logits(unscaled_logits, row_positions, column_ids):
    return jnp.where(
        column_ids[None, :] == row_positions[:, None],
        MASKED_LOGIT,
        unscaled_logits / SOFTMAX_WARMTH,
    )


def log_total(similarity_logits):
    highest = jnp.max(similarity_logits, axis=1)
    return highest + jnp.log(jnp.sum(jnp.exp(similarity_logits - highest[:, None]), axis=1))


def pair_weights(similarity_logits, row_lse, all_lse, row_positions, column_ids, partner):
    partner_rows = jnp.take(partner, row_positions)
    own_partner = (column_ids[None, :] == partner_rows[:, None]).astype(jnp.float32)
    other_partner = (partner[None, :] == row_positions[:, None]).astype(jnp.float32)
    return (
        jnp.exp(similarity_logits - row_lse[:, None])
        + jnp.exp(similarity_logits - all_lse[None, :])
        - own_partner
        - other_partner
    )


def partner_pick(similarity_logits, row_positions, column_ids, partner):
    partner_rows = jnp.take(partner, row_positions)
    return jnp.sum(
        jnp.where(column_ids[None, :] == partner_rows[:, None], similarity_logits, 0.0), axis=1
    )


def local(
    hidden_in,
    attn_gain,
    w_query,
    query_gain,
    cached_keys,
    cached_values,
    w_out,
    final_gain,
    lengths,
    pack_order,
    partner,
):
    pack_size = lax.axis_size("pack")
    pack_index = lax.axis_index("pack")
    group_index = lax.axis_index("dp")
    stmt_count, feature_count = hidden_in.shape
    model_width = feature_count * pack_size
    head_dim = query_gain.shape[0]
    local_heads = w_query.shape[1] // head_dim
    token_count = cached_keys.shape[0]
    total_stmts = partner.shape[0]
    inputs32 = hidden_in.astype(jnp.float32)
    input_squares = over_copies(jnp.sum(inputs32 * inputs32, axis=1), "pack")
    input_rms = lax.rsqrt(input_squares / model_width + EPSILON)
    normed = (inputs32 * input_rms[:, None] * attn_gain[None, :]).astype(jnp.bfloat16)
    projected = jnp.dot(collect(normed, "pack", 1), w_query, preferred_element_type=jnp.float32)
    queries = projected.reshape(stmt_count, local_heads, head_dim)
    queries = (
        queries
        * lax.rsqrt(jnp.mean(queries * queries, axis=2, keepdims=True) + EPSILON)
        * query_gain
    )
    lengths_row = lengths[0]
    order_row = pack_order[0]
    queries = rotate_heads(queries, (lengths_row - 1).astype(jnp.float32)).astype(jnp.bfloat16)
    all_queries = collect(queries, "pack", 1)
    token_owners = token_owner(lengths_row, order_row, pack_index * token_count, token_count)
    block_max, block_sum, numerators = block_attention(
        all_queries, cached_keys, cached_values, token_owners, head_dim ** (-0.5)
    )
    maxima = lax.all_to_all(
        block_max.reshape(stmt_count, pack_size, local_heads).astype(jnp.bfloat16),
        "pack",
        split_axis=1,
        concat_axis=1,
        tiled=True,
    ).astype(jnp.float32)
    totals = lax.all_to_all(
        block_sum.reshape(stmt_count, pack_size, local_heads).astype(jnp.bfloat16),
        "pack",
        split_axis=1,
        concat_axis=1,
        tiled=True,
    ).astype(jnp.float32)
    numer_parts = lax.all_to_all(
        numerators.reshape(stmt_count, pack_size, local_heads, head_dim).astype(jnp.bfloat16),
        "pack",
        split_axis=1,
        concat_axis=1,
        tiled=True,
    ).astype(jnp.float32)
    highest = jnp.max(maxima, axis=1, keepdims=True)
    factor = jnp.exp(maxima - highest)
    denominator = jnp.sum(totals * factor, axis=1)
    summed = jnp.sum(numer_parts * factor[..., None], axis=1)
    own_heads = (summed / denominator[..., None]).astype(jnp.bfloat16)
    partial_out = jnp.dot(
        own_heads.reshape(stmt_count, local_heads * head_dim),
        w_out,
        preferred_element_type=jnp.float32,
    )
    attn_out = sent_and_summed(partial_out.astype(jnp.bfloat16), "pack", 1)
    hidden = inputs32 + attn_out
    hidden_squares = over_copies(jnp.sum(hidden * hidden, axis=1), "pack")
    hidden_rms = jnp.sqrt(hidden_squares / model_width + EPSILON)
    pooled = (hidden / hidden_rms[:, None] * final_gain[None, :]).astype(jnp.bfloat16)
    pooled32 = pooled.astype(jnp.float32)
    pooled_squares = over_copies(jnp.sum(pooled32 * pooled32, axis=1), "pack")
    pooled_norm = jnp.sqrt(pooled_squares)
    premise_vectors = (pooled32 / pooled_norm[:, None]).astype(jnp.bfloat16)
    panels = collect(premise_vectors, "dp", 0)
    partial_logits = lax.dot_general(
        premise_vectors, panels, (((1,), (1,)), ((), ())), preferred_element_type=jnp.float32
    )
    column_ids = jnp.arange(total_stmts, dtype=jnp.int32)
    row_base = group_index * stmt_count
    summed_logits = total_of(partial_logits.astype(jnp.bfloat16), "pack")
    row_positions = row_base + jnp.arange(stmt_count, dtype=jnp.int32)
    similarity_logits = masked_logits(summed_logits, row_positions, column_ids)
    group_lse = log_total(similarity_logits)
    own_count = stmt_count // pack_size
    loss_group = group_lse - partner_pick(similarity_logits, row_positions, column_ids, partner)
    loss_rows = lax.dynamic_slice_in_dim(loss_group, pack_index * own_count, own_count, 0)
    all_lse = collect(group_lse, "dp", 0)
    all_weights = pair_weights(
        similarity_logits, group_lse, all_lse, row_positions, column_ids, partner
    ).astype(jnp.bfloat16)
    gathered_rows = jnp.dot(all_weights, panels, preferred_element_type=jnp.float32)
    embedding_gradient = gathered_rows / SOFTMAX_WARMTH
    embed32 = premise_vectors.astype(jnp.float32)
    inner_sum = over_copies(jnp.sum(embed32 * embedding_gradient, axis=1), "pack")
    grad_pooled = (embedding_gradient - embed32 * inner_sum[:, None]) / pooled_norm[:, None]
    grad_hidden = (
        model_width**0.5 * final_gain[None, :] * grad_pooled / hidden_rms[:, None]
    ).astype(jnp.bfloat16)
    return (pooled, loss_rows, grad_hidden)


def solution(mesh):
    in_specs = (
        P("dp", "pack"),
        P("pack"),
        P(None, "pack"),
        P(),
        P(("dp", "pack"), None),
        P(("dp", "pack"), None),
        P("pack", None),
        P("pack"),
        P("dp", None),
        P("dp", None),
        P(),
    )
    out_specs = (P("dp", "pack"), P(("dp", "pack")), P("dp", "pack"))
    return jax.shard_map(local, mesh=mesh, in_specs=in_specs, out_specs=out_specs, check_vma=False)
```

profile of v0, /device:TPU:1, one launch (start us, length us, event | category | flops | bytes accessed | tf_op | source)
XLA Modules:
  0.0 277.4 jit_solution(13439479615849610034)
XLA Ops:
  0.7 1.0 fusion.29
  1.7 18.2 %all_to_all.75 = f32[32,1,64]{2,1,0:T(1,128)S(1)} all-to-all(f32[32,1,64]{2,1,0:T(1,128)S(1)} %broadcast_in_dim.119), channel_id=1, replica_groups=mesh['dp'=16,'pack'=32] {'pack'}, dimensions={0} | all-to-all | bytes 16384 | tf_op jit(solution)/shard_map/all_to_all | solution.py:14
  19.9 0.8 fusion.31
  20.7 0.9 broadcast_in_dim.120
  21.6 4.3 %all-to-all-start.1 = ((bf16[32,64,128]{2,1,0:T(8,128)(2,1)}), bf16[32,64,128]{2,1,0:T(8,128)(2,1)S(1)}, u32[]{:S(2)}, u32[]{:S(2)}) async-start(bf16[32,64,128]{2,1,0:T(8,128)(2,1)} %broadcast_in_dim.120), calls=%async_computation.1 | async-start | bytes 1048576 | tf_op jit(solution)/shard_map/all_to_all | solution.py:14
  26.0 0.8 select_reduce_fusion.1
  27.1 1.2 copy.120
  29.4 13.3 %all-to-all-done.1 = bf16[32,64,128]{2,1,0:T(8,128)(2,1)S(1)} async-done(((bf16[32,64,128]{2,1,0:T(8,128)(2,1)}), bf16[32,64,128]{2,1,0:T(8,128)(2,1)S(1)}, u32[]{:S(2)}, u32[]{:S(2)}) %all-to-all-start.1) | async-done | bytes 524320 | tf_op jit(solution)/shard_map/all_to_all | solution.py:14
  43.4 0.9 broadcast_in_dim.121
  44.3 5.6 %all-to-all-start.2 = ((bf16[32,64,1,128]{3,1,2,0:T(8,128)(2,1)}), bf16[32,64,1,128]{3,1,2,0:T(8,128)(2,1)S(1)}, u32[]{:S(2)}, u32[]{:S(2)}) async-start(bf16[32,64,1,128]{3,1,2,0:T(8,128)(2,1)} %broadcast_in_dim.121), calls=%async_computation.2 | async-start | bytes 1048576 | tf_op jit(solution)/shard_map/all_to_all | solution.py:14
  50.0 4.4 %fusion.38 = (s32[320]{0:T(512)S(1)}, s32[320,1]{0,1:T(1,128)S(1)}) fusion(s32[]{:T(128)} %bitcast.60, s32[]{:T(128)} %bitcast.61, s32[]{:T(128)} %bitcast.62, s32[]{:T(128)} %bitcast.63, s32[]{:T(128)} %bitcast.64, s32[]{:T(128)} %bitcast.66, s32[]{:T(128)} %bitcast.65, s32[320]{0:T(512)S(1)} %convert_reduce_fusion.1), kind=kLoop, calls=%fused_computation.144 | loop fusion | flops 4800 | bytes 3868 | tf_op jit(solution)/shard_map/jit(_take)/gather | solution.py:75
  56.7 35.6 %select_select_fusion = s32[320]{0:T(512)S(1)} fusion(pred[320]{0:T(512)(128)(4,1)S(1)} %get-tuple-element.62, pred[320]{0:T(512)(128)(4,1)S(1)} %get-tuple-element.61, pred[320]{0:T(512)(128)(4,1)S(1)} %get-tuple-element.60, pred[320]{0:T(512)(128)(4,1)S(1)} %get-tuple-element.59, pred[320]{0:T(512)(128)(4,1)S(1)} %get-tuple-element.58, ...), kind=kLoop, calls=%fused_computation.141 | loop fusion | flops 20480 | bytes 22308 | tf_op jit(solution)/shard_map/jit(_take)/select_n | solution.py:75
  93.2 1.7 copy-done.2
  94.8 1.1 fusion.3
  96.6 8.4 %all-to-all-start.5 = ((bf16[64,32,1]{0,2,1:T(2,128)(2,1)}), bf16[64,32,1]{0,2,1:T(2,128)(2,1)S(1)}, u32[]{:S(2)}, u32[]{:S(2)}) async-start(bf16[64,32,1]{0,2,1:T(2,128)(2,1)} %copy.102), calls=%async_computation.5 | async-start | bytes 32768 | tf_op jit(solution)/shard_map/all_to_all | solution.py:188
  105.7 7.0 %all-to-all-done.5 = bf16[64,32,1]{0,2,1:T(2,128)(2,1)S(1)} async-done(((bf16[64,32,1]{0,2,1:T(2,128)(2,1)}), bf16[64,32,1]{0,2,1:T(2,128)(2,1)S(1)}, u32[]{:S(2)}, u32[]{:S(2)}) %all-to-all-start.5) | async-done | bytes 4128 | tf_op jit(solution)/shard_map/all_to_all | solution.py:188
  112.7 4.3 %all-to-all-start.4 = ((bf16[64,32,1]{0,2,1:T(2,128)(2,1)}), bf16[64,32,1]{0,2,1:T(2,128)(2,1)S(1)}, u32[]{:S(2)}, u32[]{:S(2)}) async-start(bf16[64,32,1]{0,2,1:T(2,128)(2,1)} %copy.101), calls=%async_computation.4 | async-start | bytes 32768 | tf_op jit(solution)/shard_map/all_to_all | solution.py:181
  117.0 3.6 %fusion.11 = bf16[8,64,4,128]{3,1,2,0:T(8,128)(2,1)} fusion(f32[8,64,4,320]{3,1,2,0:T(8,128)} %copy-done.2, f32[64,8,4]{0,2,1:T(4,128)S(1)} %get-tuple-element.139, pred[64,320]{1,0:T(8,128)(4,1)S(1)} %iota_compare_fusion.2, bf16[320,8,128,1]{2,1,0,3:T(8,128)(2,1)S(1)} %bitcast.147), kind=kOutput, calls=%fused_computation.14 | convolution fusion | flops 170655744 | bytes 3829760 | tf_op jit(solution)/shard_map/skgt,tkd->skgd/dot_general | solution.py:95
  120.6 4.3 %all-to-all-done.4 = bf16[64,32,1]{0,2,1:T(2,128)(2,1)S(1)} async-done(((bf16[64,32,1]{0,2,1:T(2,128)(2,1)}), bf16[64,32,1]{0,2,1:T(2,128)(2,1)S(1)}, u32[]{:S(2)}, u32[]{:S(2)}) %all-to-all-start.4) | async-done | bytes 4128 | tf_op jit(solution)/shard_map/all_to_all | solution.py:181
  124.9 4.3 %all-to-all-start.3 = ((bf16[64,32,1,128]{3,0,2,1:T(8,128)(2,1)}), bf16[64,32,1,128]{3,0,2,1:T(8,128)(2,1)S(1)}, u32[]{:S(2)}, u32[]{:S(2)}) async-start(bf16[64,32,1,128]{3,0,2,1:T(8,128)(2,1)} %bitcast.79), calls=%async_computation.3 | async-start | bytes 1048576 | tf_op jit(solution)/shard_map/all_to_all | solution.py:195
  129.4 16.6 %all-to-all-done.3 = bf16[64,32,1,128]{3,0,2,1:T(8,128)(2,1)S(1)} async-done(((bf16[64,32,1,128]{3,0,2,1:T(8,128)(2,1)}), bf16[64,32,1,128]{3,0,2,1:T(8,128)(2,1)S(1)}, u32[]{:S(2)}, u32[]{:S(2)}) %all-to-all-start.3) | async-done | bytes 524320 | tf_op jit(solution)/shard_map/all_to_all | solution.py:195
  146.8 21.4 %all_to_all.76 = bf16[32,64,128]{2,1,0:T(8,128)(2,1)S(1)} all-to-all(bf16[32,64,128]{2,1,0:T(8,128)(2,1)S(1)} %bitcast.144), channel_id=1, replica_groups=mesh['dp'=16,'pack'=32] {'pack'}, dimensions={0} | all-to-all | bytes 1048576 | tf_op jit(solution)/shard_map/all_to_all | solution.py:39
  168.5 12.6 %all_to_all.77 = f32[32,1,64]{2,1,0:T(1,128)S(1)} all-to-all(f32[32,1,64]{2,1,0:T(1,128)S(1)} %broadcast_in_dim.124), channel_id=1, replica_groups=mesh['dp'=16,'pack'=32] {'pack'}, dimensions={0} | all-to-all | bytes 16384 | tf_op jit(solution)/shard_map/all_to_all | solution.py:14
  181.4 11.4 %all_to_all.78 = f32[32,1,64]{2,1,0:T(1,128)S(1)} all-to-all(f32[32,1,64]{2,1,0:T(1,128)S(1)} %broadcast_in_dim.126), channel_id=1, replica_groups=mesh['dp'=16,'pack'=32] {'pack'}, dimensions={0} | all-to-all | bytes 16384 | tf_op jit(solution)/shard_map/all_to_all | solution.py:14
  193.0 23.5 %all_to_all.79 = bf16[16,64,128]{2,1,0:T(8,128)(2,1)S(1)} all-to-all(bf16[16,64,128]{2,1,0:T(8,128)(2,1)S(1)} %broadcast_in_dim.127), channel_id=1, replica_groups=mesh['dp'=16,'pack'=32] {'dp'}, dimensions={0} | all-to-all | bytes 524288 | tf_op jit(solution)/shard_map/all_to_all | solution.py:14
  217.4 5.6 %all-to-all-start.10 = ((bf16[32,2,1024]{2,1,0:T(2,128)(2,1)}), bf16[32,2,1024]{2,1,0:T(2,128)(2,1)S(1)}, u32[]{:S(2)}, u32[]{:S(2)}) async-start(bf16[32,2,1024]{2,1,0:T(2,128)(2,1)} %reshape.359), calls=%async_computation.10 | async-start | bytes 262144 | tf_op jit(solution)/shard_map/all_to_all | solution.py:39
  223.8 8.4 %all-to-all-done.10 = bf16[32,2,1024]{2,1,0:T(2,128)(2,1)S(1)} async-done(((bf16[32,2,1024]{2,1,0:T(2,128)(2,1)}), bf16[32,2,1024]{2,1,0:T(2,128)(2,1)S(1)}, u32[]{:S(2)}, u32[]{:S(2)}) %all-to-all-start.10) | async-done | bytes 131104 | tf_op jit(solution)/shard_map/all_to_all | solution.py:39
  233.0 5.1 %all-to-all-start.11 = ((bf16[32,2,1024]{2,1,0:T(2,128)(2,1)}), bf16[32,2,1024]{2,1,0:T(2,128)(2,1)S(1)}, u32[]{:S(2)}, u32[]{:S(2)}) async-start(bf16[32,2,1024]{2,1,0:T(2,128)(2,1)} %broadcast_in_dim.128), calls=%async_computation.11 | async-start | bytes 262144 | tf_op jit(solution)/shard_map/all_to_all | solution.py:14
  238.4 9.0 %all-to-all-done.11 = bf16[32,2,1024]{2,1,0:T(2,128)(2,1)S(1)} async-done(((bf16[32,2,1024]{2,1,0:T(2,128)(2,1)}), bf16[32,2,1024]{2,1,0:T(2,128)(2,1)S(1)}, u32[]{:S(2)}, u32[]{:S(2)}) %all-to-all-start.11) | async-done | bytes 131104 | tf_op jit(solution)/shard_map/all_to_all | solution.py:14
  248.0 11.7 %all_to_all.80 = f32[16,1,64]{2,1,0:T(1,128)S(1)} all-to-all(f32[16,1,64]{2,1,0:T(1,128)S(1)} %broadcast_in_dim.130), channel_id=1, replica_groups=mesh['dp'=16,'pack'=32] {'dp'}, dimensions={0} | all-to-all | bytes 8192 | tf_op jit(solution)/shard_map/all_to_all | solution.py:14
  262.3 6.5 %all-to-all-start.13 = ((f32[32,1,64]{2,1,0:T(1,128)}), f32[32,1,64]{2,1,0:T(1,128)S(1)}, u32[]{:S(2)}, u32[]{:S(2)}) async-start(f32[32,1,64]{2,1,0:T(1,128)} %broadcast_in_dim.131), calls=%async_computation.13 | async-start | bytes 32768 | tf_op jit(solution)/shard_map/all_to_all | solution.py:14
  269.6 7.1 %all-to-all-done.13 = f32[32,1,64]{2,1,0:T(1,128)S(1)} async-done(((f32[32,1,64]{2,1,0:T(1,128)}), f32[32,1,64]{2,1,0:T(1,128)S(1)}, u32[]{:S(2)}, u32[]{:S(2)}) %all-to-all-start.13) | async-done | bytes 8224 | tf_op jit(solution)/shard_map/all_to_all | solution.py:14
  (98 shorter events, 15.6 us)
Async XLA Ops:
  0.6 145.7 %copy-start = (bf16[128,4096]{1,0:T(8,128)(2,1)S(1)}, bf16[128,4096]{1,0:T(8,128)(2,1)}, u32[]{:S(2)}) copy-start(bf16[128,4096]{1,0:T(8,128)(2,1)} %param.19) | copy-start | bytes 3145732
  0.6 28.6 %copy-start.10 = (s32[1,64]{1,0:T(1,128)S(1)}, s32[1,64]{1,0:T(1,128)}, u32[]{:S(2)}) copy-start(s32[1,64]{1,0:T(1,128)} %param.21) | copy-start | bytes 772
  0.7 27.7 %copy-start.3 = (s32[1,64]{1,0:T(1,128)S(1)}, s32[1,64]{1,0:T(1,128)}, u32[]{:S(2)}) copy-start(s32[1,64]{1,0:T(1,128)} %param.22) | copy-start | bytes 772
  0.7 42.0 %copy-start.4 = (bf16[4096,128]{1,0:T(8,128)(2,1)S(1)}, bf16[4096,128]{1,0:T(8,128)(2,1)}, u32[]{:S(2)}) copy-start(bf16[4096,128]{1,0:T(8,128)(2,1)} %param.15) | copy-start | bytes 3145732
  0.7 42.5 %copy-start.8 = (f32[128]{0:T(128)S(1)}, f32[128]{0:T(128)}, u32[]{:S(2)}) copy-start(f32[128]{0:T(128)} %param.16) | copy-start | bytes 1540
  21.6 21.1 %all-to-all-start.1 = ((bf16[32,64,128]{2,1,0:T(8,128)(2,1)}), bf16[32,64,128]{2,1,0:T(8,128)(2,1)S(1)}, u32[]{:S(2)}, u32[]{:S(2)}) async-start(bf16[32,64,128]{2,1,0:T(8,128)(2,1)} %broadcast_in_dim.120), calls=%async_computation.1 | async-start | bytes 1048576 | tf_op jit(solution)/shard_map/all_to_all | solution.py:14
  44.3 48.1 %all-to-all-start.2 = ((bf16[32,64,1,128]{3,1,2,0:T(8,128)(2,1)}), bf16[32,64,1,128]{3,1,2,0:T(8,128)(2,1)S(1)}, u32[]{:S(2)}, u32[]{:S(2)}) async-start(bf16[32,64,1,128]{3,1,2,0:T(8,128)(2,1)} %broadcast_in_dim.121), calls=%async_computation.2 | async-start | bytes 1048576 | tf_op jit(solution)/shard_map/all_to_all | solution.py:14
  92.4 12.6 %copy-start.5 = (bf16[320,1024]{1,0:T(8,128)(2,1)S(1)}, bf16[320,1024]{1,0:T(8,128)(2,1)}, u32[]{:S(2)}) copy-start(bf16[320,1024]{1,0:T(8,128)(2,1)} %param.18) | copy-start | bytes 1966084
  93.2 1.7 copy-start.2
  96.6 16.2 %all-to-all-start.5 = ((bf16[64,32,1]{0,2,1:T(2,128)(2,1)}), bf16[64,32,1]{0,2,1:T(2,128)(2,1)S(1)}, u32[]{:S(2)}, u32[]{:S(2)}) async-start(bf16[64,32,1]{0,2,1:T(2,128)(2,1)} %copy.102), calls=%async_computation.5 | async-start | bytes 32768 | tf_op jit(solution)/shard_map/all_to_all | solution.py:188
  112.7 12.2 %all-to-all-start.4 = ((bf16[64,32,1]{0,2,1:T(2,128)(2,1)}), bf16[64,32,1]{0,2,1:T(2,128)(2,1)S(1)}, u32[]{:S(2)}, u32[]{:S(2)}) async-start(bf16[64,32,1]{0,2,1:T(2,128)(2,1)} %copy.101), calls=%async_computation.4 | async-start | bytes 32768 | tf_op jit(solution)/shard_map/all_to_all | solution.py:181
  120.6 47.8 %copy-start.6 = (bf16[64,128]{1,0:T(8,128)(2,1)S(1)}, bf16[64,128]{1,0:T(8,128)(2,1)}, u32[]{:S(2)}) copy-start(bf16[64,128]{1,0:T(8,128)(2,1)} %param.13) | copy-start | bytes 49156
  120.6 60.6 %copy-start.9 = (f32[128]{0:T(128)S(1)}, f32[128]{0:T(128)}, u32[]{:S(2)}) copy-start(f32[128]{0:T(128)} %param.20) | copy-start | bytes 1540
  124.9 21.1 %all-to-all-start.3 = ((bf16[64,32,1,128]{3,0,2,1:T(8,128)(2,1)}), bf16[64,32,1,128]{3,0,2,1:T(8,128)(2,1)S(1)}, u32[]{:S(2)}, u32[]{:S(2)}) async-start(bf16[64,32,1,128]{3,0,2,1:T(8,128)(2,1)} %bitcast.79), calls=%async_computation.3 | async-start | bytes 1048576 | tf_op jit(solution)/shard_map/all_to_all | solution.py:195
  146.3 76.7 %copy-start.1 = (s32[1024]{0:T(1024)S(1)}, s32[1024]{0:T(1024)}, u32[]{:S(2)}) copy-start(s32[1024]{0:T(1024)} %param.23) | copy-start | bytes 12292
  181.4 96.0 %copy-start.7 = (bf16[64,128]{1,0:T(8,128)(2,1)}, bf16[64,128]{1,0:T(8,128)(2,1)S(1)}, u32[]{:S(2)}) copy-start(bf16[64,128]{1,0:T(8,128)(2,1)S(1)} %get-tuple-element.64) | copy-start | bytes 49156
  217.4 14.8 %all-to-all-start.10 = ((bf16[32,2,1024]{2,1,0:T(2,128)(2,1)}), bf16[32,2,1024]{2,1,0:T(2,128)(2,1)S(1)}, u32[]{:S(2)}, u32[]{:S(2)}) async-start(bf16[32,2,1024]{2,1,0:T(2,128)(2,1)} %reshape.359), calls=%async_computation.10 | async-start | bytes 262144 | tf_op jit(solution)/shard_map/all_to_all | solution.py:39
  233.0 14.3 %all-to-all-start.11 = ((bf16[32,2,1024]{2,1,0:T(2,128)(2,1)}), bf16[32,2,1024]{2,1,0:T(2,128)(2,1)S(1)}, u32[]{:S(2)}, u32[]{:S(2)}) async-start(bf16[32,2,1024]{2,1,0:T(2,128)(2,1)} %broadcast_in_dim.128), calls=%async_computation.11 | async-start | bytes 262144 | tf_op jit(solution)/shard_map/all_to_all | solution.py:14
  262.3 14.4 %all-to-all-start.13 = ((f32[32,1,64]{2,1,0:T(1,128)}), f32[32,1,64]{2,1,0:T(1,128)S(1)}, u32[]{:S(2)}, u32[]{:S(2)}) async-start(f32[32,1,64]{2,1,0:T(1,128)} %broadcast_in_dim.131), calls=%async_computation.13 | async-start | bytes 32768 | tf_op jit(solution)/shard_map/all_to_all | solution.py:14
where the time goes:
time: 279 us; the launch traced here: 277 us
  blocking collectives  98.8 us (35%)
  waiting for transfers between devices  65.6 us (24%)
  other arithmetic  48 us (17%)
  starting transfers between devices  44.3 us (16%)
  local copies, waits for them, and re-layouts  14 us (5%)
  matrix products  5.58 us (2%)
    all_to_all x5, blocking collectives, from_everyone(): return lax.all_to_all(copies, axis, split_axis=0, concat_axis=0, tiled=True)  77.4 us
    select_n x1, other arithmetic, token_owner(): return jnp.take(order_row, slot_index)  35.6 us
    all_to_all x4, waiting for transfers between devices, from_everyone(): return lax.all_to_all(copies, axis, split_axis=0, concat_axis=0, tiled=True)  29.3 us
    all_to_all x4, starting transfers between devices, from_everyone(): return lax.all_to_all(copies, axis, split_axis=0, concat_axis=0, tiled=True)  21.6 us
    all_to_all x1, blocking collectives, sent_and_summed(): lax.all_to_all(tiles, axis, split_axis=0, concat_axis=0, tiled=True)  21.4 us
    all_to_all x1, waiting for transfers between devices, local(): lax.all_to_all(numerators.reshape(stmt_count, pack_size, local_heads, hea...  16.6 us
    all_to_all x1, starting transfers between devices, local(): lax.all_to_all(block_sum.reshape(stmt_count, pack_size, local_heads).asty...  8.42 us
    all_to_all x1, waiting for transfers between devices, sent_and_summed(): lax.all_to_all(tiles, axis, split_axis=0, concat_axis=0, tiled=True)  8.39 us
  transfers between devices with their start and end apart: 8, of which 7 were waited for; matrix products, arithmetic and copies ran while one was open for 19% of the time, Pallas kernels for 0%

commit v1 on v0

v1 whole, which is shorter than its diff:
```python
import math

import jax
import jax.numpy as jnp
from jax import lax
from jax.experimental import pallas as pl
from jax.experimental.pallas import tpu as pltpu
from jax.sharding import PartitionSpec as P

EPSILON = 1e-06
WARMTH = 0.05
ROPE_BASE = 1000000.0
MASKED = -1e30
F32 = jnp.float32
BF16 = jnp.bfloat16
I32 = jnp.int32

SLOTS = 24
STAT = SLOTS - 1
PACK = 32
CHIPS = 16
DP = 16
MESH = pl.DeviceIdType.MESH


def far_first(k, half):
    return half + (1 - 2 * lax.rem(k, 2)) * lax.div(k + 1, 2)


def dot_t(a, b):
    return lax.dot_general(a, b, (((1,), (1,)), ((), ())), preferred_element_type=F32)


def dot(a, b):
    return jnp.dot(a, b, preferred_element_type=F32)


def iota(shape, dim):
    return lax.broadcasted_iota(I32, shape, dim)


def kernel(
    hid_ref, again_ref, wq_hbm, qgain_ref, k_hbm, v_hbm, wo_hbm, fgain_ref, len_ref, ord_ref, part_ref,
    pooled_ref, loss_ref, grad_ref,
    x_ref, wq, kk, vv, wo, msg, ints, selbig, sel, bias, cosr, sinr,
    sq, qb, ob_out, ob, att, po_out, po_in, pb, st_own, st_in, ds_own, ds_in,
    pls, lb, lb_in, ub, ls_own, ls_in, uf,
    load_sem, x_send, x_recv, f_send, f_recv, ss, rs,
):
    g = lax.axis_index("dp")
    p = lax.axis_index("pack")
    z, y, c = lax.div(p, 16), lax.div(lax.rem(p, 16), 2), lax.rem(p, 2)
    sib = p + 1 - 2 * c
    chip = z * 8 + y
    n_stmt = hid_ref.shape[0]

    def pack_peer(i):
        k, r = lax.div(i, 4), lax.rem(i, 4)
        py = lax.rem(y + far_first(k, 4), 8)
        pz = lax.rem(z + 1 - lax.div(r, 2), 2)
        pc = lax.rem(c + 1 - lax.rem(r, 2), 2)
        return pz * 16 + py * 2 + pc

    def chip_peer(i):
        k = lax.div(i, 2)
        py = lax.rem(y + far_first(k, 4), 8)
        pz = lax.rem(z + 1 - lax.rem(i, 2), 2)
        return pz * 8 + py

    gx, gz = lax.div(g, 4), lax.rem(g, 4)

    def dp_peer(i):
        a, b = lax.div(i, 4), lax.rem(i, 4)
        return lax.rem(gx + far_first(a, 2), 4) * 4 + lax.rem(gz + far_first(b, 2), 4)

    def remote(src, dst, send, recv, dg, dp_):
        return pltpu.make_async_remote_copy(
            src_ref=src, dst_ref=dst, send_sem=send, recv_sem=recv,
            device_id=(dg, dp_), device_id_type=MESH,
        )

    loads = [
        pltpu.make_async_copy(wq_hbm.at[:, 0], wq.at[0], load_sem.at[0]),
        pltpu.make_async_copy(wq_hbm.at[:, 1], wq.at[1], load_sem.at[1]),
        pltpu.make_async_copy(k_hbm, kk, load_sem.at[2]),
        pltpu.make_async_copy(v_hbm, vv, load_sem.at[3]),
        pltpu.make_async_copy(wo_hbm, wo.at[c], load_sem.at[4]),
    ]
    barrier = pltpu.get_barrier_semaphore()

    def greet_pack(i, carry):
        pl.semaphore_signal(barrier, inc=1, device_id=(g, pack_peer(i)), device_id_type=MESH)
        return carry

    def greet_dp(i, carry):
        pl.semaphore_signal(barrier, inc=1, device_id=(dp_peer(i), p), device_id_type=MESH)
        return carry

    lax.fori_loop(0, DP - 1, greet_dp, 0)
    lax.fori_loop(0, PACK - 1, greet_pack, 0)
    for load in loads:
        load.start()

    lane = iota((n_stmt, 128), 1)
    sub = iota((n_stmt, 128), 0)
    same = lane == sub
    lane1 = iota((1, 128), 1)

    def to_row(col):
        return jnp.sum(jnp.where(same, col, 0.0), axis=0, keepdims=True)

    def to_col(row):
        return jnp.sum(jnp.where(same, row, 0.0), axis=1, keepdims=True)

    h32 = hid_ref[...].astype(F32)
    msg[0:n_stmt, :] = (h32 * again_ref[...]).astype(BF16)
    sq_row = to_row(jnp.sum(h32 * h32, axis=1, keepdims=True))
    sq_hi = sq_row.astype(BF16).astype(F32)
    row16 = iota((16, 128), 0)
    msg[n_stmt:, :] = jnp.where(
        row16 == 0, sq_hi, jnp.where(row16 == 1, sq_row - sq_hi, 0.0)
    ).astype(BF16)

    row8 = iota((8, 128), 0)
    ints[...] = jnp.where(row8 == 1, -1.0, 0.0)
    ints[0:1, 0:n_stmt] = len_ref[...].astype(F32)
    ints[1:2, 0:n_stmt] = ord_ref[...].astype(F32)
    len_row = ints[0:1, :]
    ord_row = ints[1:2, :]
    len_col = to_col(len_row)
    lane_f = lane.astype(F32)
    sub_f = sub.astype(F32)
    at = sub_f == ord_row
    plen_row = jnp.sum(jnp.where(at, len_col, 0.0), axis=0, keepdims=True)
    plen_col = to_col(plen_row)
    end_row = jnp.sum(jnp.where(sub <= lane, plen_col, 0.0), axis=0, keepdims=True)
    start_row = end_row - plen_row
    place_col = jnp.sum(jnp.where(at, lane_f, 0.0), axis=1, keepdims=True)
    place_row = jnp.where(lane1 < n_stmt, to_row(place_col), -1000.0)
    start_col = jnp.sum(jnp.where(at, start_row, 0.0), axis=1, keepdims=True)
    end_col = jnp.sum(jnp.where(at, end_row, 0.0), axis=1, keepdims=True)
    tokens = float(k_hbm.shape[0])
    end_real = jnp.where(lane1 < n_stmt, end_row, 1e9)

    def before(tok):
        return jnp.sum(jnp.where(end_real <= tok, 1.0, 0.0), axis=1, keepdims=True)

    b3 = iota((PACK, SLOTS, 128), 0).reshape(PACK * SLOTS, 128).astype(F32)
    j3 = iota((PACK, SLOTS, 128), 1).reshape(PACK * SLOTS, 128).astype(F32)
    first_big = before(b3 * tokens)
    selbig[...] = jnp.where(place_row == first_big + j3, 1.0, 0.0).astype(BF16)

    block_a = jnp.floor((start_col + 0.5) * (1.0 / tokens))
    block_b = jnp.floor((end_col - 0.5) * (1.0 / tokens))
    slot_a = place_col - before(block_a * tokens)
    slot_b = place_col - before(block_b * tokens)
    wide = iota((n_stmt, PACK * SLOTS), 1).astype(F32)
    for i, (blk, slot) in enumerate(
        ((block_a, slot_a), (block_b, slot_b), (block_a, float(STAT)), (block_b, float(STAT)))
    ):
        sel[i * n_stmt:(i + 1) * n_stmt, :] = jnp.where(
            wide == blk * SLOTS + slot, 1.0, 0.0
        ).astype(BF16)

    pf = p.astype(F32)
    slot_id = before(jnp.zeros((SLOTS, 128), F32) + pf * tokens) + iota((SLOTS, 1), 0).astype(F32)
    lane24 = iota((SLOTS, 128), 1).astype(F32)
    st = jnp.sum(jnp.where(lane24 == slot_id, start_row, 0.0), axis=1, keepdims=True)
    en = jnp.sum(jnp.where(lane24 == slot_id, end_row, 0.0), axis=1, keepdims=True)
    tok = iota((SLOTS, k_hbm.shape[0]), 1).astype(F32) + pf * tokens
    own_bias = jnp.where((tok >= st) & (tok < en), 0.0, MASKED)
    for i in range(4):
        bias[i * SLOTS:(i + 1) * SLOTS, :] = own_bias

    freq = jnp.exp(
        jnp.where(lane1 < 64, lane1, lane1 - 64).astype(F32) * (-2.0 / 128.0 * math.log(ROPE_BASE))
    )
    angle = (len_col - 1.0) * freq
    cosr[...] = jnp.cos(angle)
    sinr[...] = jnp.where(lane < 64, -1.0, 1.0) * jnp.sin(angle)

    pl.semaphore_wait(barrier, PACK - 1 + DP - 1)

    def x_cols(ch):
        return pl.ds(pl.multiple_of(ch * 128, 128), 128)

    def x_start(i, carry):
        to = chip_peer(i)
        remote(msg, x_ref.at[c, :, x_cols(chip)], x_send, x_recv.at[14 - i], g, to * 2 + c).start()
        return carry

    lax.fori_loop(0, CHIPS - 1, x_start, 0)
    remote(msg, x_ref.at[c, :, x_cols(chip)], f_send, f_recv, g, sib).start()
    x_ref[c, :, x_cols(chip)] = msg[...]

    def source_chip(i):
        k = lax.div(i, 2)
        py = lax.rem(y + 8 - far_first(k, 4), 8)
        pz = lax.rem(z + 1 - lax.rem(i, 2), 2)
        return pz * 8 + py

    def x_forward(n, carry):
        src = source_chip(14 - n)
        view = x_ref.at[c, :, x_cols(src)]
        remote(view, view, x_send, x_recv.at[n], g, p).wait_recv()
        remote(view, view, f_send, f_recv, g, sib).start()
        return carry

    lax.fori_loop(0, CHIPS - 1, x_forward, 0)
    w_copy = remote(wo_hbm, wo.at[c], ss.at[0], rs.at[0], g, sib)
    loads[0].wait()
    loads[1].wait()
    q_own = dot(x_ref[c, 0:n_stmt, :], wq[c].reshape(CHIPS * 128, 128))
    f_all = x_ref.at[1 - c]
    remote(f_all, f_all, f_send, f_recv, g, sib).wait_recv()
    q_raw = q_own + dot(x_ref[1 - c, 0:n_stmt, :], wq[1 - c].reshape(CHIPS * 128, 128))
    sq_sum = jnp.zeros((16, 128), F32)
    for i in range(2):
        for j in range(CHIPS):
            sq_sum = sq_sum + x_ref[i, n_stmt:, j * 128:(j + 1) * 128].astype(F32)
    total = to_col(sq_sum[0:1, :] + sq_sum[1:2, :])
    mean_sq = jnp.sum(q_raw * q_raw, axis=1, keepdims=True) * (1.0 / 128.0)
    inv = lax.rsqrt(mean_sq + EPSILON * (total * (1.0 / (PACK * 128)) + EPSILON))
    q = q_raw * inv * qgain_ref[...]
    q = (q * cosr[...] + pltpu.roll(q, 64, 1) * sinr[...]).astype(BF16)
    q128 = jnp.concatenate([q, jnp.zeros((128 - n_stmt, 128), BF16)], axis=0)
    sq[...] = dot(selbig[...], q128).astype(BF16).reshape(PACK, SLOTS, 128)

    def q_start(i, carry):
        to = pack_peer(i)
        remote(sq.at[to], qb.at[p], ss.at[1], rs.at[1], g, to).start()
        return carry

    lax.fori_loop(0, PACK - 1, q_start, 0)
    qb[p] = sq[p]
    w_copy.start()
    loads[2].wait()
    loads[3].wait()
    q31 = qb.at[0:PACK - 1]
    remote(q31, q31, ss.at[1], rs.at[1], g, sib).wait_recv()

    scale = 128 ** -0.5
    jr = iota((SLOTS, 128), 0)
    jl = iota((SLOTS, 128), 1)
    for n in range(8):
        dj = (2, 1, 3, 0)[n // 2]
        kz = lax.rem(z + 1 - n % 2, 2)
        kh = kz * 4 + lax.rem(lax.div(y, 2) + dj, 4)
        cols = pl.ds(pl.multiple_of(kh * 128, 128), 128)
        qs = qb[pl.ds(kh * 4, 4)].reshape(4 * SLOTS, 128)
        s = dot_t(qs, kk[:, cols]) * scale + bias[...]
        m = jnp.max(s, axis=1, keepdims=True)
        w = jnp.exp(s - m)
        l = jnp.sum(w, axis=1, keepdims=True)
        o = dot(w.astype(BF16), vv[:, cols]) / l
        lse = m + jnp.log(l)
        hi = lse.astype(BF16).astype(F32)
        mid = (lse - hi).astype(BF16).astype(F32)
        lo = lse - hi - mid
        for r in range(4):
            part = slice(r * SLOTS, (r + 1) * SLOTS)
            stat = jnp.where(
                jl == jr, hi[part], jnp.where(
                    jl == jr + 32, mid[part], jnp.where(jl == jr + 64, lo[part], 0.0)
                )
            )
            stat = jnp.sum(stat, axis=0, keepdims=True)
            ob_out[kh * 4 + r] = jnp.where(jr == STAT, stat, o[part]).astype(BF16)
        if n < 7:
            for r in range(4):
                to = kh * 4 + r
                remote(ob_out.at[to], ob.at[p], ss.at[2], rs.at[2], g, to).start()
        else:
            for r in range(1, 4):
                to = kh * 4 + lax.rem(lax.rem(p, 4) + r, 4)
                remote(ob_out.at[to], ob.at[p], ss.at[2], rs.at[2], g, to).start()
    ob[p] = ob_out[p]
    o31 = ob.at[0:PACK - 1]
    remote(o31, o31, ss.at[2], rs.at[2], g, sib).wait_recv()

    got = dot(sel[...], ob[...].reshape(PACK * SLOTS, 128))

    def stat_of(rows, slot):
        hit = (lane_f == slot) | (lane_f == slot + 32.0) | (lane_f == slot + 64.0)
        return jnp.sum(jnp.where(hit, rows, 0.0), axis=1, keepdims=True)

    lse_a = stat_of(got[2 * n_stmt:3 * n_stmt], slot_a)
    lse_b = stat_of(got[3 * n_stmt:], slot_b)
    top = jnp.maximum(lse_a, lse_b)
    w_a = jnp.exp(lse_a - top)
    w_b = jnp.where(block_a == block_b, 0.0, jnp.exp(lse_b - top))
    own_att = ((w_a * got[0:n_stmt] + w_b * got[n_stmt:2 * n_stmt]) / (w_a + w_b)).astype(BF16)
    att[c] = own_att
    remote(att.at[c], att.at[c], ss.at[3], rs.at[3], g, sib).start()
    loads[4].wait()
    w_copy.wait_recv()
    remote(att.at[c], att.at[1 - c], ss.at[3], rs.at[3], g, sib).wait_recv()
    heads = jnp.concatenate([att[0], att[1]], axis=1)
    for i in range(CHIPS):
        to = chip_peer(i)
        cols = pl.ds(pl.multiple_of((to * 2 + c) * 128, 128), 128)
        w2 = jnp.concatenate([wo[0, :, cols], wo[1, :, cols]], axis=0)
        part = dot(heads, w2)
        if i < CHIPS - 1:
            po_out[i] = part.astype(BF16)
            remote(po_out.at[i], po_in.at[i], ss.at[4], rs.at[4], g, to * 2 + c).start()
        else:
            own_part = part
    remote(po_out, po_in, ss.at[4], rs.at[4], g, sib).wait_recv()
    hid = hid_ref[...].astype(F32) + own_part
    for i in range(CHIPS - 1):
        hid = hid + po_in[i].astype(F32)

    fgain = fgain_ref[...]
    feat = (hid * fgain).astype(BF16)
    pb[g] = feat
    f32feat = feat.astype(F32)

    def p_start(i, carry):
        remote(pb.at[g], pb.at[g], ss.at[5], rs.at[5], dp_peer(i), p).start()
        return carry

    lax.fori_loop(0, DP - 1, p_start, 0)
    s1 = jnp.sum(hid * hid, axis=1, keepdims=True)
    s2 = jnp.sum(f32feat * f32feat, axis=1, keepdims=True)
    st_row = jnp.sum(
        jnp.where(same, s1, 0.0) + jnp.where(lane == sub + 64, s2, 0.0), axis=0, keepdims=True
    )
    st_own[...] = st_row
    st_in[p] = st_row

    def s_start(i, carry):
        remote(st_own, st_in.at[p], ss.at[6], rs.at[6], g, pack_peer(i)).start()
        return carry

    lax.fori_loop(0, PACK - 1, s_start, 0)
    s31 = st_in.at[0:PACK - 1]
    remote(s31, s31, ss.at[6], rs.at[6], g, sib).wait_recv()
    st_row = jnp.sum(st_in[...], axis=0)
    odd = lax.rem(g, 2)
    half_row = lax.div(g, 2)
    in_half = lax.div(lane1, 64) == odd

    def own_half(row):
        return jnp.where(in_half, jnp.where(odd == 1, row, pltpu.roll(row, 64, 1)), 0.0)

    ds_own[...] = own_half(st_row)
    ds_in[odd, half_row] = ds_own[...]

    def d_start(i, carry):
        remote(ds_own, ds_in.at[odd, half_row], ss.at[7], rs.at[7], dp_peer(i), p).start()
        return carry

    lax.fori_loop(0, DP - 1, d_start, 0)
    s1_all = to_col(jnp.where(lane1 < 64, st_row, 0.0))
    s2_all = to_col(jnp.where(lane1 < 64, pltpu.roll(st_row, 64, 1), 0.0))
    inv_norm = lax.rsqrt(s2_all)
    rms = jnp.sqrt(s1_all * (1.0 / (PACK * 128)) + EPSILON)
    pooled_ref[...] = (hid / rms * fgain).astype(BF16)
    p15 = pb.at[0:DP - 1]
    remote(p15, p15, ss.at[5], rs.at[5], g, sib).wait_recv()

    for j in range(8):
        cols = pb[2 * j:2 * j + 2].reshape(128, 128)
        pls[pl.ds(j, n_stmt, stride=8), :] = dot_t(feat, cols)
    lb[...] = pls[...].astype(BF16).reshape(PACK, 16, 128)

    def l_start(i, carry):
        to = pack_peer(i)
        remote(lb.at[to], lb_in.at[p], ss.at[8], rs.at[8], g, to).start()
        return carry

    lax.fori_loop(0, PACK - 1, l_start, 0)
    lb_in[p] = lb[p]
    dall = st_in.at[0:DP - 1]
    remote(dall, dall, ss.at[7], rs.at[7], g, sib).wait_recv()
    inv_all = lax.rsqrt((ds_in[0] + ds_in[1]).reshape(8, 128))
    l31 = lb_in.at[0:PACK - 1]
    remote(l31, l31, ss.at[8], rs.at[8], g, sib).wait_recv()
    acc = jnp.zeros((16, 128), F32)
    for i in range(PACK):
        acc = acc + lb_in[i].astype(F32)
    col_id = iota((8, 128), 0) * 128 + iota((8, 128), 1)
    partner = part_ref[...]

    def whole(x):
        return jnp.sum(jnp.sum(x, axis=1, keepdims=True), axis=0, keepdims=True)

    losses = []
    exps = []
    for i in range(2):
        row_id = g * n_stmt + p * 2 + i
        diag = col_id == row_id
        own_inv = whole(jnp.where(diag, inv_all, 0.0))
        logit = acc[8 * i:8 * i + 8] * inv_all * (own_inv * (1.0 / WARMTH))
        e = jnp.where(diag, 0.0, jnp.exp(logit))
        own_partner = whole(jnp.where(diag, partner.astype(F32), 0.0))
        target = whole(jnp.where(col_id.astype(F32) == own_partner, logit, 0.0))
        losses.append(jnp.log(whole(e)) - target)
        exps.append(e)
    lane2 = iota((1, 2), 1)
    loss_ref[...] = jnp.where(lane2 == 0, losses[0], losses[1])
    ub[p] = jnp.concatenate(exps, axis=0).astype(BF16)

    def u_start(i, carry):
        remote(ub.at[p], ub.at[p], ss.at[9], rs.at[9], g, pack_peer(i)).start()
        return carry

    lax.fori_loop(0, PACK - 1, u_start, 0)
    u31 = ub.at[0:PACK - 1]
    remote(u31, u31, ss.at[9], rs.at[9], g, sib).wait_recv()
    uf[...] = ub[...].reshape(PACK * 16, 128).astype(F32)
    mats = [uf[pl.ds(j, n_stmt, stride=8), :] for j in range(8)]
    row_sum = mats[0]
    for j in range(1, 8):
        row_sum = row_sum + mats[j]
    inv_sum = 1.0 / jnp.sum(row_sum, axis=1, keepdims=True)
    inv_row = jnp.sum(jnp.where(lane == sub + 64, inv_sum, 0.0), axis=0, keepdims=True)
    ls_own[...] = own_half(inv_row)
    ls_in[odd, half_row] = ls_own[...]

    def e_start(i, carry):
        remote(ls_own, ls_in.at[odd, half_row], ss.at[10], rs.at[10], dp_peer(i), p).start()
        return carry

    lax.fori_loop(0, DP - 1, e_start, 0)
    row_f = (g * n_stmt + iota((n_stmt, 1), 0)).astype(F32)
    part_f = partner.astype(F32)
    own_part_col = jnp.zeros((n_stmt, 1), F32)
    for j in range(8):
        own_part_col = own_part_col + jnp.sum(
            jnp.where((lane + 128 * j).astype(F32) == row_f, part_f[j:j + 1, :], 0.0), axis=1, keepdims=True
        )
    pairs = []
    logs = []
    for j in range(8):
        cid = (lane + 128 * j).astype(F32)
        pairs.append(
            jnp.where(cid == own_part_col, 1.0, 0.0) + jnp.where(part_f[j:j + 1, :] == row_f, 1.0, 0.0)
        )
        logs.append(jnp.log(jnp.maximum(mats[j], 1e-30)))
    remote(dall, dall, ss.at[10], rs.at[10], g, sib).wait_recv()
    sums_all = (ls_in[0] + ls_in[1]).reshape(8, 128)
    grad = jnp.zeros((n_stmt, 128), F32)
    inner_acc = jnp.zeros((n_stmt, 128), F32)
    for j in range(8):
        wj = mats[j] * (inv_sum + sums_all[j:j + 1, :]) - pairs[j]
        inner_acc = inner_acc + wj * logs[j]
        grad = grad + dot(
            (wj * inv_all[j:j + 1, :]).astype(BF16), pb[2 * j:2 * j + 2].reshape(128, 128)
        )
    inner = jnp.sum(inner_acc, axis=1, keepdims=True)
    out = grad * (1.0 / WARMTH) - f32feat * (inv_norm * inner)
    grad_ref[...] = (out * fgain * (inv_norm * float(PACK * 128) ** 0.5)).astype(BF16)

    x15 = x_ref.at[0, :, 0:(CHIPS - 1) * 128]
    remote(x15, x15, x_send, f_recv, g, sib).wait_send()
    remote(f_all, f_all, f_send, f_recv, g, sib).wait_send()
    w_copy.wait_send()
    for i, view in ((1, q31), (2, o31), (3, att.at[0]), (4, po_out), (5, p15), (6, s31), (7, dall), (8, l31), (9, u31), (10, dall)):
        remote(view, view, ss.at[i], rs.at[i], g, sib).wait_send()


def local(
    hidden_in, attn_gain, w_query, query_gain, cached_keys, cached_values, w_out, final_gain,
    lengths, pack_order, partner,
):
    n = hidden_in.shape[0]
    toks, kvw = cached_keys.shape
    width = w_query.shape[0]
    vmem = pl.BlockSpec(memory_space=pltpu.VMEM)
    hbm = pl.BlockSpec(memory_space=pl.ANY)
    V = pltpu.VMEM
    dma = pltpu.SemaphoreType.DMA
    pooled, loss, grad = pl.pallas_call(
        kernel,
        out_shape=(
            jax.ShapeDtypeStruct((n, 128), BF16),
            jax.ShapeDtypeStruct((1, 2), F32),
            jax.ShapeDtypeStruct((n, 128), BF16),
        ),
        in_specs=[vmem, vmem, hbm, vmem, hbm, hbm, hbm, vmem, vmem, vmem, vmem],
        out_specs=(vmem, vmem, vmem),
        scratch_shapes=[
            V((2, n + 16, CHIPS * 128), BF16),
            V((2, CHIPS, 128, 128), BF16),
            V((toks, kvw), BF16),
            V((toks, kvw), BF16),
            V((2, 128, width), BF16),
            V((n + 16, 128), BF16),
            V((8, 128), F32),
            V((PACK * SLOTS, 128), BF16),
            V((4 * n, PACK * SLOTS), BF16),
            V((4 * SLOTS, toks), F32),
            V((n, 128), F32),
            V((n, 128), F32),
            V((PACK, SLOTS, 128), BF16),
            V((PACK, SLOTS, 128), BF16),
            V((PACK, SLOTS, 128), BF16),
            V((PACK, SLOTS, 128), BF16),
            V((2, n, 128), BF16),
            V((CHIPS - 1, n, 128), BF16),
            V((CHIPS - 1, n, 128), BF16),
            V((DP, n, 128), BF16),
            V((1, 128), F32),
            V((PACK, 1, 128), F32),
            V((1, 128), F32),
            V((2, 8, 1, 128), F32),
            V((n * 8, 128), F32),
            V((PACK, 16, 128), BF16),
            V((PACK, 16, 128), BF16),
            V((PACK, 16, 128), BF16),
            V((1, 128), F32),
            V((2, 8, 1, 128), F32),
            V((n * 8, 128), F32),
            dma((5,)),
            dma(()),
            dma((CHIPS - 1,)),
            dma(()),
            dma(()),
            dma((11,)),
            dma((11,)),
        ],
        compiler_params=pltpu.CompilerParams(
            collective_id=0, has_side_effects=True, vmem_limit_bytes=48 * 1024 * 1024
        ),
    )(
        hidden_in,
        attn_gain.reshape(1, 128),
        w_query.reshape(CHIPS, 2, 128, 128),
        query_gain.reshape(1, 128),
        cached_keys,
        cached_values,
        w_out,
        final_gain.reshape(1, 128),
        lengths,
        pack_order,
        partner.reshape(8, 128),
    )
    return pooled, loss.reshape(2), grad


def solution(mesh):
    in_specs = (
        P("dp", "pack"),
        P("pack"),
        P(None, "pack"),
        P(),
        P(("dp", "pack"), None),
        P(("dp", "pack"), None),
        P("pack", None),
        P("pack"),
        P("dp", None),
        P("dp", None),
        P(),
    )
    out_specs = (P("dp", "pack"), P(("dp", "pack")), P("dp", "pack"))
    return jax.shard_map(local, mesh=mesh, in_specs=in_specs, out_specs=out_specs, check_vma=False)
```

time: 279 us -> 87 us (0.31)
  blocking collectives: 98.8 us -> 0 us
  Pallas kernels: 0 us -> 78.2 us
  waiting for transfers between devices: 65.6 us -> 0 us
  other arithmetic: 48 us -> 0 us
  starting transfers between devices: 44.3 us -> 0 us
  local copies, waits for them, and re-layouts: 14 us -> 7.75 us
  matrix products: 5.58 us -> 0 us
    all_to_all x6 -> x0, blocking collectives: 98.8 us -> none  [the longest x5 77.4 us: from_everyone(): return lax.all_to_all(copies, axis, split_axis=0, concat_axis=0, tiled=True)]
    pallas_call x0 -> x1, Pallas kernels: none -> 78.2 us  [local(): pl.pallas_call(kernel, out_shape=(jax.ShapeDtypeStruct((n, 128), BF16), j...]
    all_to_all x8 -> x0, waiting for transfers between devices: 65.6 us -> none  [the longest x4 29.3 us: from_everyone(): return lax.all_to_all(copies, axis, split_axis=0, concat_axis=0, tiled=True)]
    all_to_all x8 -> x0, starting transfers between devices: 44.3 us -> none  [the longest x4 21.6 us: from_everyone(): return lax.all_to_all(copies, axis, split_axis=0, concat_axis=0, tiled=True)]
    select_n x3 -> x0, other arithmetic: 35.6 us -> none  [the longest x1 35.6 us: token_owner(): return jnp.take(order_row, slot_index)]
    dot_general x6 -> x0, matrix products: 5.58 us -> none  [the longest x1 3.57 us: block_attention(): jnp.einsum('skgt,tkd->skgd', softmax_weights.astype(jnp.bfloat16), value_...]
    unnamed x24 -> x25, local copies, waits for them, and re-layouts: 3.05 us -> 7.75 us
    gather x3 -> x0, other arithmetic: 4.66 us -> none  [the longest x2 4.65 us: token_owner(): return jnp.take(order_row, slot_index)]
  transfers between devices with their start and end apart: 8 -> 0, of which waited for: 7 -> 0; matrix products, arithmetic and copies ran while one was open for 19% -> 0% of each run, Pallas kernels for 0% -> 0%
where the time goes in v1:
time: 87 us; the launch traced here: 86.7 us
  Pallas kernels  78.2 us (90%)
  local copies, waits for them, and re-layouts  7.75 us (9%)
    pallas_call x1, Pallas kernels, local(): pl.pallas_call(kernel, out_shape=(jax.ShapeDtypeStruct((n, 128), BF16), j...  78.2 us
    unnamed x25, local copies, waits for them, and re-layouts  7.75 us

profile of v1, /device:TPU:1, one launch (start us, length us, event | category | flops | bytes accessed | tf_op | source)
XLA Modules:
  0.0 86.7 jit_solution(5182864299746441131)
XLA Ops:
  0.6 0.0 copy-start.5
  0.6 0.0 copy-start.9
  0.7 0.0 copy-start.10
  0.7 0.0 copy-start.6
  0.7 0.0 copy-start.7
  0.7 0.0 copy-start.8
  0.7 0.6 copy-done.5
  1.3 0.0 copy-done.9
  1.3 0.0 copy-done.10
  1.3 0.0 copy-done.6
  1.3 0.0 copy-done.7
  1.4 0.0 copy-done.8
  1.4 0.0 copy-start
  1.4 1.2 %copy-done = bf16[4096,128]{1,0:T(8,128)(2,1)S(1)} copy-done((bf16[4096,128]{1,0:T(8,128)(2,1)S(1)}, bf16[4096,128]{1,0:T(8,128)(2,1)}, u32[]{:S(2)}) %copy-start) | copy-done | bytes 1048600
  2.6 0.0 copy-start.1
  2.6 1.2 %copy-done.1 = bf16[128,4096]{1,0:T(8,128)(2,1)S(1)} copy-done((bf16[128,4096]{1,0:T(8,128)(2,1)S(1)}, bf16[128,4096]{1,0:T(8,128)(2,1)}, u32[]{:S(2)}) %copy-start.1) | copy-done | bytes 1048600
  3.8 0.0 copy-start.2
  3.8 1.1 %copy-done.2 = bf16[320,1024]{1,0:T(8,128)(2,1)S(1)} copy-done((bf16[320,1024]{1,0:T(8,128)(2,1)S(1)}, bf16[320,1024]{1,0:T(8,128)(2,1)}, u32[]{:S(2)}) %copy-start.2) | copy-done | bytes 655384
  4.9 0.0 copy-start.3
  4.9 1.1 %copy-done.3 = bf16[320,1024]{1,0:T(8,128)(2,1)S(1)} copy-done((bf16[320,1024]{1,0:T(8,128)(2,1)S(1)}, bf16[320,1024]{1,0:T(8,128)(2,1)}, u32[]{:S(2)}) %copy-start.3) | copy-done | bytes 655384
  6.0 0.0 copy-start.4
  6.0 0.7 copy-done.4
  6.7 78.2 %shard_map.130 = (bf16[64,128]{1,0:T(8,128)(2,1)S(1)}, f32[1,2]{1,0:T(1,128)S(1)}, bf16[64,128]{1,0:T(8,128)(2,1)S(1)}) custom-call(bf16[64,128]{1,0:T(8,128)(2,1)S(1)} %copy-done.4, f32[1,128]{1,0:T(1,128)S(1)} %bitcast.8, bf16[16,2,128,128]{3,2,1,0:T(8,128)(2,1)S(1)} %bitcast.6, f32[1,128]{1,0:T(1,128)S(1)} %bitcast.9, bf16[320,1024]{1,0:T(8,128)(2,1)S(1)} %copy-done.2, ...), custom_call_target="tpu_custom_call" | custom-call | tf_op jit(solution)/shard_map/pallas_call | solution.py:475
  84.9 0.6 copy.17
  85.6 0.5 copy.18
  86.1 0.6 copy.19
Async XLA Ops:
  0.6 0.7 copy-start.5
  0.6 0.7 copy-start.9
  0.7 0.7 copy-start.10
  0.7 0.7 copy-start.6
  0.7 0.7 copy-start.7
  0.7 0.7 copy-start.8
  1.4 1.2 %copy-start = (bf16[4096,128]{1,0:T(8,128)(2,1)S(1)}, bf16[4096,128]{1,0:T(8,128)(2,1)}, u32[]{:S(2)}) copy-start(bf16[4096,128]{1,0:T(8,128)(2,1)} %param.13) | copy-start | bytes 3145732
  2.6 1.2 %copy-start.1 = (bf16[128,4096]{1,0:T(8,128)(2,1)S(1)}, bf16[128,4096]{1,0:T(8,128)(2,1)}, u32[]{:S(2)}) copy-start(bf16[128,4096]{1,0:T(8,128)(2,1)} %wo_hbm.1) | copy-start | bytes 3145732
  3.8 1.1 %copy-start.2 = (bf16[320,1024]{1,0:T(8,128)(2,1)S(1)}, bf16[320,1024]{1,0:T(8,128)(2,1)}, u32[]{:S(2)}) copy-start(bf16[320,1024]{1,0:T(8,128)(2,1)} %k_hbm.1) | copy-start | bytes 1966084
  4.9 1.1 %copy-start.3 = (bf16[320,1024]{1,0:T(8,128)(2,1)S(1)}, bf16[320,1024]{1,0:T(8,128)(2,1)}, u32[]{:S(2)}) copy-start(bf16[320,1024]{1,0:T(8,128)(2,1)} %v_hbm.1) | copy-start | bytes 1966084
  6.0 0.7 copy-start.4

commit v2 on v1

--- a/solution.py
+++ b/solution.py
@@ -24,7 +24,12 @@
 
 
 def far_first(k, half):
-    return half + (1 - 2 * lax.rem(k, 2)) * lax.div(k + 1, 2)
+    return half + (1 - 2 * (k % 2)) * ((k + 1) // 2)
+
+
+def each(n, step):
+    for i in range(n):
+        step(i)
 
 
 def dot_t(a, b):
@@ -42,10 +47,10 @@
 def kernel(
     hid_ref, again_ref, wq_hbm, qgain_ref, k_hbm, v_hbm, wo_hbm, fgain_ref, len_ref, ord_ref, part_ref,
     pooled_ref, loss_ref, grad_ref,
-    x_ref, wq, kk, vv, wo, msg, ints, selbig, sel, bias, cosr, sinr,
+    x_ref, qx, wq, kk, vv, wo, msg, ints, selbig, sel, bias, cosr, sinr,
     sq, qb, ob_out, ob, att, po_out, po_in, pb, st_own, st_in, ds_own, ds_in,
     pls, lb, lb_in, ub, ls_own, ls_in, uf,
-    load_sem, x_send, x_recv, f_send, f_recv, ss, rs,
+    load_sem, ss, rs, x_recv,
 ):
     g = lax.axis_index("dp")
     p = lax.axis_index("pack")
@@ -55,22 +60,21 @@
     n_stmt = hid_ref.shape[0]
 
     def pack_peer(i):
-        k, r = lax.div(i, 4), lax.rem(i, 4)
+        k, r = i // 4, i % 4
         py = lax.rem(y + far_first(k, 4), 8)
-        pz = lax.rem(z + 1 - lax.div(r, 2), 2)
-        pc = lax.rem(c + 1 - lax.rem(r, 2), 2)
+        pz = (z, 1 - z)[1 - r // 2]
+        pc = (c, 1 - c)[1 - r % 2]
         return pz * 16 + py * 2 + pc
 
     def chip_peer(i):
-        k = lax.div(i, 2)
-        py = lax.rem(y + far_first(k, 4), 8)
-        pz = lax.rem(z + 1 - lax.rem(i, 2), 2)
+        py = lax.rem(y + far_first(i // 2, 4), 8)
+        pz = (z, 1 - z)[1 - i % 2]
         return pz * 8 + py
 
     gx, gz = lax.div(g, 4), lax.rem(g, 4)
 
     def dp_peer(i):
-        a, b = lax.div(i, 4), lax.rem(i, 4)
+        a, b = i // 4, i % 4
         return lax.rem(gx + far_first(a, 2), 4) * 4 + lax.rem(gz + far_first(b, 2), 4)
 
     def remote(src, dst, send, recv, dg, dp_):
@@ -79,25 +83,23 @@
             device_id=(dg, dp_), device_id_type=MESH,
         )
 
+    pending = []
     loads = [
-        pltpu.make_async_copy(wq_hbm.at[:, 0], wq.at[0], load_sem.at[0]),
-        pltpu.make_async_copy(wq_hbm.at[:, 1], wq.at[1], load_sem.at[1]),
-        pltpu.make_async_copy(k_hbm, kk, load_sem.at[2]),
-        pltpu.make_async_copy(v_hbm, vv, load_sem.at[3]),
-        pltpu.make_async_copy(wo_hbm, wo.at[c], load_sem.at[4]),
+        pltpu.make_async_copy(wq_hbm.at[:, c], wq.at[c], load_sem.at[0]),
+        pltpu.make_async_copy(k_hbm, kk, load_sem.at[1]),
+        pltpu.make_async_copy(v_hbm, vv, load_sem.at[2]),
+        pltpu.make_async_copy(wo_hbm, wo.at[c], load_sem.at[3]),
     ]
     barrier = pltpu.get_barrier_semaphore()
 
-    def greet_pack(i, carry):
+    def greet_pack(i):
         pl.semaphore_signal(barrier, inc=1, device_id=(g, pack_peer(i)), device_id_type=MESH)
-        return carry
-
-    def greet_dp(i, carry):
+
+    def greet_dp(i):
         pl.semaphore_signal(barrier, inc=1, device_id=(dp_peer(i), p), device_id_type=MESH)
-        return carry
-
-    lax.fori_loop(0, DP - 1, greet_dp, 0)
-    lax.fori_loop(0, PACK - 1, greet_pack, 0)
+
+    each(DP - 1, greet_dp)
+    each(PACK - 1, greet_pack)
     for load in loads:
         load.start()
 
@@ -112,16 +114,31 @@
     def to_col(row):
         return jnp.sum(jnp.where(same, row, 0.0), axis=1, keepdims=True)
 
+    row8 = iota((8, 128), 0)
     h32 = hid_ref[...].astype(F32)
     msg[0:n_stmt, :] = (h32 * again_ref[...]).astype(BF16)
     sq_row = to_row(jnp.sum(h32 * h32, axis=1, keepdims=True))
     sq_hi = sq_row.astype(BF16).astype(F32)
-    row16 = iota((16, 128), 0)
     msg[n_stmt:, :] = jnp.where(
-        row16 == 0, sq_hi, jnp.where(row16 == 1, sq_row - sq_hi, 0.0)
+        row8 == 0, sq_hi, jnp.where(row8 == 1, sq_row - sq_hi, 0.0)
     ).astype(BF16)
 
-    row8 = iota((8, 128), 0)
+    pl.semaphore_wait(barrier, PACK - 1 + DP - 1)
+
+    wq_copy = remote(wq_hbm.at[:, 1 - c], wq.at[c], ss.at[11], rs.at[11], g, sib)
+
+    def x_start(i):
+        remote(msg, x_ref.at[i], ss.at[0], x_recv.at[i // 4], g, chip_peer(i) * 2 + c).start()
+
+    def source_chip(i):
+        py = lax.rem(y + 8 - far_first(i // 2, 4), 8)
+        pz = (z, 1 - z)[1 - i % 2]
+        return pz * 8 + py
+
+    each(CHIPS - 1, x_start)
+    wq_copy.start()
+    x_ref[CHIPS - 1] = msg[...]
+
     ints[...] = jnp.where(row8 == 1, -1.0, 0.0)
     ints[0:1, 0:n_stmt] = len_ref[...].astype(F32)
     ints[1:2, 0:n_stmt] = ord_ref[...].astype(F32)
@@ -179,45 +196,34 @@
     cosr[...] = jnp.cos(angle)
     sinr[...] = jnp.where(lane < 64, -1.0, 1.0) * jnp.sin(angle)
 
-    pl.semaphore_wait(barrier, PACK - 1 + DP - 1)
-
-    def x_cols(ch):
-        return pl.ds(pl.multiple_of(ch * 128, 128), 128)
-
-    def x_start(i, carry):
-        to = chip_peer(i)
-        remote(msg, x_ref.at[c, :, x_cols(chip)], x_send, x_recv.at[14 - i], g, to * 2 + c).start()
-        return carry
-
-    lax.fori_loop(0, CHIPS - 1, x_start, 0)
-    remote(msg, x_ref.at[c, :, x_cols(chip)], f_send, f_recv, g, sib).start()
-    x_ref[c, :, x_cols(chip)] = msg[...]
-
-    def source_chip(i):
-        k = lax.div(i, 2)
-        py = lax.rem(y + 8 - far_first(k, 4), 8)
-        pz = lax.rem(z + 1 - lax.rem(i, 2), 2)
-        return pz * 8 + py
-
-    def x_forward(n, carry):
-        src = source_chip(14 - n)
-        view = x_ref.at[c, :, x_cols(src)]
-        remote(view, view, x_send, x_recv.at[n], g, p).wait_recv()
-        remote(view, view, f_send, f_recv, g, sib).start()
-        return carry
-
-    lax.fori_loop(0, CHIPS - 1, x_forward, 0)
-    w_copy = remote(wo_hbm, wo.at[c], ss.at[0], rs.at[0], g, sib)
+    w_copy = remote(wo_hbm, wo.at[c], ss.at[13], rs.at[13], g, sib)
     loads[0].wait()
-    loads[1].wait()
-    q_own = dot(x_ref[c, 0:n_stmt, :], wq[c].reshape(CHIPS * 128, 128))
-    f_all = x_ref.at[1 - c]
-    remote(f_all, f_all, f_send, f_recv, g, sib).wait_recv()
-    q_raw = q_own + dot(x_ref[1 - c, 0:n_stmt, :], wq[1 - c].reshape(CHIPS * 128, 128))
-    sq_sum = jnp.zeros((16, 128), F32)
-    for i in range(2):
-        for j in range(CHIPS):
-            sq_sum = sq_sum + x_ref[i, n_stmt:, j * 128:(j + 1) * 128].astype(F32)
+    x15 = x_ref.at[0:CHIPS - 1]
+    wq_copy.wait_recv()
+    pending.append(remote(x15, x15, ss.at[0], rs.at[0], g, sib).wait_send)
+    pending.append(wq_copy.wait_send)
+    parts = [jnp.zeros((n_stmt, 128), F32), jnp.zeros((n_stmt, 128), F32)]
+    sq_sum = jnp.zeros((8, 128), F32)
+    for k in (3, 2, 1, 0):
+        group = x_ref.at[4 * k:min(4 * k + 4, CHIPS - 1)]
+        remote(group, group, ss.at[0], x_recv.at[k], g, sib).wait_recv()
+        slots = list(range(4 * k, 4 * k + 4))
+        blocks = jnp.concatenate([x_ref[i, 0:n_stmt, :] for i in slots], axis=1)
+        for i in slots:
+            sq_sum = sq_sum + x_ref[i, n_stmt:, :].astype(F32)
+        for h in range(2):
+            head = (1 - c, c)[h]
+            weights = jnp.concatenate([wq[head, source_chip(i)] for i in slots], axis=0)
+            parts[h] = parts[h] + dot(blocks, weights)
+            if k == 0 and h == 0:
+                qx[0, 0:n_stmt, :] = parts[0]
+                qx[0, n_stmt:, :] = sq_sum
+                q_copy = remote(qx.at[0], qx.at[1], ss.at[12], rs.at[12], g, sib)
+                q_copy.start()
+                pending.append(q_copy.wait_send)
+    q_copy.wait_recv()
+    q_raw = parts[1] + qx[1, 0:n_stmt, :]
+    sq_sum = sq_sum + qx[1, n_stmt:, :]
     total = to_col(sq_sum[0:1, :] + sq_sum[1:2, :])
     mean_sq = jnp.sum(q_raw * q_raw, axis=1, keepdims=True) * (1.0 / 128.0)
     inv = lax.rsqrt(mean_sq + EPSILON * (total * (1.0 / (PACK * 128)) + EPSILON))
@@ -226,17 +232,18 @@
     q128 = jnp.concatenate([q, jnp.zeros((128 - n_stmt, 128), BF16)], axis=0)
     sq[...] = dot(selbig[...], q128).astype(BF16).reshape(PACK, SLOTS, 128)
 
-    def q_start(i, carry):
+    def q_start(i):
         to = pack_peer(i)
         remote(sq.at[to], qb.at[p], ss.at[1], rs.at[1], g, to).start()
-        return carry
-
-    lax.fori_loop(0, PACK - 1, q_start, 0)
+
+    each(PACK - 1, q_start)
     qb[p] = sq[p]
     w_copy.start()
+    loads[1].wait()
     loads[2].wait()
-    loads[3].wait()
     q31 = qb.at[0:PACK - 1]
+    pending.append(remote(q31, q31, ss.at[1], rs.at[1], g, sib).wait_send)
+    pending.append(w_copy.wait_send)
     remote(q31, q31, ss.at[1], rs.at[1], g, sib).wait_recv()
 
     scale = 128 ** -0.5
@@ -244,7 +251,7 @@
     jl = iota((SLOTS, 128), 1)
     for n in range(8):
         dj = (2, 1, 3, 0)[n // 2]
-        kz = lax.rem(z + 1 - n % 2, 2)
+        kz = (z, 1 - z)[1 - n % 2]
         kh = kz * 4 + lax.rem(lax.div(y, 2) + dj, 4)
         cols = pl.ds(pl.multiple_of(kh * 128, 128), 128)
         qs = qb[pl.ds(kh * 4, 4)].reshape(4 * SLOTS, 128)
@@ -276,6 +283,7 @@
                 remote(ob_out.at[to], ob.at[p], ss.at[2], rs.at[2], g, to).start()
     ob[p] = ob_out[p]
     o31 = ob.at[0:PACK - 1]
+    pending.append(remote(o31, o31, ss.at[2], rs.at[2], g, sib).wait_send)
     remote(o31, o31, ss.at[2], rs.at[2], g, sib).wait_recv()
 
     got = dot(sel[...], ob[...].reshape(PACK * SLOTS, 128))
@@ -292,7 +300,8 @@
     own_att = ((w_a * got[0:n_stmt] + w_b * got[n_stmt:2 * n_stmt]) / (w_a + w_b)).astype(BF16)
     att[c] = own_att
     remote(att.at[c], att.at[c], ss.at[3], rs.at[3], g, sib).start()
-    loads[4].wait()
+    pending.append(remote(att.at[c], att.at[c], ss.at[3], rs.at[3], g, sib).wait_send)
+    loads[3].wait()
     w_copy.wait_recv()
     remote(att.at[c], att.at[1 - c], ss.at[3], rs.at[3], g, sib).wait_recv()
     heads = jnp.concatenate([att[0], att[1]], axis=1)
@@ -306,6 +315,7 @@
             remote(po_out.at[i], po_in.at[i], ss.at[4], rs.at[4], g, to * 2 + c).start()
         else:
             own_part = part
+    pending.append(remote(po_out, po_in, ss.at[4], rs.at[4], g, sib).wait_send)
     remote(po_out, po_in, ss.at[4], rs.at[4], g, sib).wait_recv()
     hid = hid_ref[...].astype(F32) + own_part
     for i in range(CHIPS - 1):
@@ -316,11 +326,10 @@
     pb[g] = feat
     f32feat = feat.astype(F32)
 
-    def p_start(i, carry):
+    def p_start(i):
         remote(pb.at[g], pb.at[g], ss.at[5], rs.at[5], dp_peer(i), p).start()
-        return carry
-
-    lax.fori_loop(0, DP - 1, p_start, 0)
+
+    each(DP - 1, p_start)
     s1 = jnp.sum(hid * hid, axis=1, keepdims=True)
     s2 = jnp.sum(f32feat * f32feat, axis=1, keepdims=True)
     st_row = jnp.sum(
@@ -329,12 +338,14 @@
     st_own[...] = st_row
     st_in[p] = st_row
 
-    def s_start(i, carry):
+    def s_start(i):
         remote(st_own, st_in.at[p], ss.at[6], rs.at[6], g, pack_peer(i)).start()
-        return carry
-
-    lax.fori_loop(0, PACK - 1, s_start, 0)
+
+    each(PACK - 1, s_start)
     s31 = st_in.at[0:PACK - 1]
+    pending.append(remote(s31, s31, ss.at[6], rs.at[6], g, sib).wait_send)
+    p15 = pb.at[0:DP - 1]
+    pending.append(remote(p15, p15, ss.at[5], rs.at[5], g, sib).wait_send)
     remote(s31, s31, ss.at[6], rs.at[6], g, sib).wait_recv()
     st_row = jnp.sum(st_in[...], axis=0)
     odd = lax.rem(g, 2)
@@ -347,17 +358,17 @@
     ds_own[...] = own_half(st_row)
     ds_in[odd, half_row] = ds_own[...]
 
-    def d_start(i, carry):
+    def d_start(i):
         remote(ds_own, ds_in.at[odd, half_row], ss.at[7], rs.at[7], dp_peer(i), p).start()
-        return carry
-
-    lax.fori_loop(0, DP - 1, d_start, 0)
+
+    each(DP - 1, d_start)
+    dall = st_in.at[0:DP - 1]
+    pending.append(remote(dall, dall, ss.at[7], rs.at[7], g, sib).wait_send)
     s1_all = to_col(jnp.where(lane1 < 64, st_row, 0.0))
     s2_all = to_col(jnp.where(lane1 < 64, pltpu.roll(st_row, 64, 1), 0.0))
     inv_norm = lax.rsqrt(s2_all)
     rms = jnp.sqrt(s1_all * (1.0 / (PACK * 128)) + EPSILON)
     pooled_ref[...] = (hid / rms * fgain).astype(BF16)
-    p15 = pb.at[0:DP - 1]
     remote(p15, p15, ss.at[5], rs.at[5], g, sib).wait_recv()
 
     for j in range(8):
@@ -365,17 +376,16 @@
         pls[pl.ds(j, n_stmt, stride=8), :] = dot_t(feat, cols)
     lb[...] = pls[...].astype(BF16).reshape(PACK, 16, 128)
 
-    def l_start(i, carry):
+    def l_start(i):
         to = pack_peer(i)
         remote(lb.at[to], lb_in.at[p], ss.at[8], rs.at[8], g, to).start()
-        return carry
-
-    lax.fori_loop(0, PACK - 1, l_start, 0)
+
+    each(PACK - 1, l_start)
     lb_in[p] = lb[p]
-    dall = st_in.at[0:DP - 1]
     remote(dall, dall, ss.at[7], rs.at[7], g, sib).wait_recv()
     inv_all = lax.rsqrt((ds_in[0] + ds_in[1]).reshape(8, 128))
     l31 = lb_in.at[0:PACK - 1]
+    pending.append(remote(l31, l31, ss.at[8], rs.at[8], g, sib).wait_send)
     remote(l31, l31, ss.at[8], rs.at[8], g, sib).wait_recv()
     acc = jnp.zeros((16, 128), F32)
     for i in range(PACK):
@@ -402,12 +412,12 @@
     loss_ref[...] = jnp.where(lane2 == 0, losses[0], losses[1])
     ub[p] = jnp.concatenate(exps, axis=0).astype(BF16)
 
-    def u_start(i, carry):
+    def u_start(i):
         remote(ub.at[p], ub.at[p], ss.at[9], rs.at[9], g, pack_peer(i)).start()
-        return carry
-
-    lax.fori_loop(0, PACK - 1, u_start, 0)
+
+    each(PACK - 1, u_start)
     u31 = ub.at[0:PACK - 1]
+    pending.append(remote(u31, u31, ss.at[9], rs.at[9], g, sib).wait_send)
     remote(u31, u31, ss.at[9], rs.at[9], g, sib).wait_recv()
     uf[...] = ub[...].reshape(PACK * 16, 128).astype(F32)
     mats = [uf[pl.ds(j, n_stmt, stride=8), :] for j in range(8)]
@@ -419,11 +429,10 @@
     ls_own[...] = own_half(inv_row)
     ls_in[odd, half_row] = ls_own[...]
 
-    def e_start(i, carry):
+    def e_start(i):
         remote(ls_own, ls_in.at[odd, half_row], ss.at[10], rs.at[10], dp_peer(i), p).start()
-        return carry
-
-    lax.fori_loop(0, DP - 1, e_start, 0)
+
+    each(DP - 1, e_start)
     row_f = (g * n_stmt + iota((n_stmt, 1), 0)).astype(F32)
     part_f = partner.astype(F32)
     own_part_col = jnp.zeros((n_stmt, 1), F32)
@@ -439,6 +448,7 @@
             jnp.where(cid == own_part_col, 1.0, 0.0) + jnp.where(part_f[j:j + 1, :] == row_f, 1.0, 0.0)
         )
         logs.append(jnp.log(jnp.maximum(mats[j], 1e-30)))
+    pending.append(remote(dall, dall, ss.at[10], rs.at[10], g, sib).wait_send)
     remote(dall, dall, ss.at[10], rs.at[10], g, sib).wait_recv()
     sums_all = (ls_in[0] + ls_in[1]).reshape(8, 128)
     grad = jnp.zeros((n_stmt, 128), F32)
@@ -453,12 +463,8 @@
     out = grad * (1.0 / WARMTH) - f32feat * (inv_norm * inner)
     grad_ref[...] = (out * fgain * (inv_norm * float(PACK * 128) ** 0.5)).astype(BF16)
 
-    x15 = x_ref.at[0, :, 0:(CHIPS - 1) * 128]
-    remote(x15, x15, x_send, f_recv, g, sib).wait_send()
-    remote(f_all, f_all, f_send, f_recv, g, sib).wait_send()
-    w_copy.wait_send()
-    for i, view in ((1, q31), (2, o31), (3, att.at[0]), (4, po_out), (5, p15), (6, s31), (7, dall), (8, l31), (9, u31), (10, dall)):
-        remote(view, view, ss.at[i], rs.at[i], g, sib).wait_send()
+    for wait in pending:
+        wait()
 
 
 def local(
@@ -469,7 +475,7 @@
     toks, kvw = cached_keys.shape
     width = w_query.shape[0]
     vmem = pl.BlockSpec(memory_space=pltpu.VMEM)
-    hbm = pl.BlockSpec(memory_space=pl.ANY)
+    hbm = pl.BlockSpec(memory_space=pltpu.HBM)
     V = pltpu.VMEM
     dma = pltpu.SemaphoreType.DMA
     pooled, loss, grad = pl.pallas_call(
@@ -482,12 +488,13 @@
         in_specs=[vmem, vmem, hbm, vmem, hbm, hbm, hbm, vmem, vmem, vmem, vmem],
         out_specs=(vmem, vmem, vmem),
         scratch_shapes=[
-            V((2, n + 16, CHIPS * 128), BF16),
+            V((CHIPS, n + 8, 128), BF16),
+            V((2, n + 8, 128), F32),
             V((2, CHIPS, 128, 128), BF16),
             V((toks, kvw), BF16),
             V((toks, kvw), BF16),
             V((2, 128, width), BF16),
-            V((n + 16, 128), BF16),
+            V((n + 8, 128), BF16),
             V((8, 128), F32),
             V((PACK * SLOTS, 128), BF16),
             V((4 * n, PACK * SLOTS), BF16),
@@ -513,16 +520,13 @@
             V((1, 128), F32),
             V((2, 8, 1, 128), F32),
             V((n * 8, 128), F32),
-            dma((5,)),
-            dma(()),
-            dma((CHIPS - 1,)),
-            dma(()),
-            dma(()),
-            dma((11,)),
-            dma((11,)),
+            dma((4,)),
+            dma((14,)),
+            dma((14,)),
+            dma((4,)),
         ],
         compiler_params=pltpu.CompilerParams(
-            collective_id=0, has_side_effects=True, vmem_limit_bytes=48 * 1024 * 1024
+            collective_id=0, has_side_effects=True
         ),
     )(
         hidden_in,

time: 87 us -> 81.5 us (0.937)
  local copies, waits for them, and re-layouts: 7.75 us -> 2.45 us
    unnamed x25 -> x7, local copies, waits for them, and re-layouts: 7.75 us -> 2.45 us
where the time goes in v2:
time: 81.5 us; the launch traced here: 81.3 us
  Pallas kernels  78.2 us (96%)
  local copies, waits for them, and re-layouts  2.45 us (3%)
    pallas_call x1, Pallas kernels, local(): pl.pallas_call(kernel, out_shape=(jax.ShapeDtypeStruct((n, 128), BF16), j...  78.2 us
    unnamed x7, local copies, waits for them, and re-layouts  2.45 us

profile of v2, /device:TPU:1, one launch (start us, length us, event | category | flops | bytes accessed | tf_op | source)
XLA Modules:
  0.0 81.3 jit_solution(9403194129024927289)
XLA Ops:
  0.6 78.2 %shard_map.130 = (bf16[64,128]{1,0:T(8,128)(2,1)}, f32[1,2]{1,0:T(1,128)}, bf16[64,128]{1,0:T(8,128)(2,1)}) custom-call(bf16[64,128]{1,0:T(8,128)(2,1)} %hid_ref.1, f32[1,128]{1,0:T(1,128)} %bitcast.8, bf16[16,2,128,128]{3,2,1,0:T(8,128)(2,1)} %bitcast.6, f32[1,128]{1,0:T(1,128)} %bitcast.9, bf16[320,1024]{1,0:T(8,128)(2,1)} %k_hbm.1, ...), custom_call_target="tpu_custom_call" | custom-call | tf_op jit(solution)/shard_map/pallas_call | solution.py:481
  78.8 0.0 copy-start.1
  78.8 0.0 copy-start
  78.8 1.3 %copy.17 = bf16[64,128]{1,0:T(8,128)(2,1)} copy(bf16[64,128]{1,0:T(8,128)(2,1)} %get-tuple-element.12) | data formatting | bytes 32768
  80.2 0.0 copy-done.1
  80.2 0.5 copy.18
  80.7 0.0 copy-done
  80.7 0.6 copy.19
Async XLA Ops:
  78.8 1.4 %copy-start.1 = (f32[1,2]{1,0:T(1,128)S(1)}, f32[1,2]{1,0:T(1,128)}, u32[]{:S(2)}) copy-start(f32[1,2]{1,0:T(1,128)} %get-tuple-element.7) | copy-start | bytes 28
  78.8 1.9 %copy-start = (bf16[64,128]{1,0:T(8,128)(2,1)S(1)}, bf16[64,128]{1,0:T(8,128)(2,1)}, u32[]{:S(2)}) copy-start(bf16[64,128]{1,0:T(8,128)(2,1)} %get-tuple-element.14) | copy-start | bytes 49156

commit v3 on v2

--- a/solution.py
+++ b/solution.py
@@ -46,11 +46,11 @@
 
 def kernel(
     hid_ref, again_ref, wq_hbm, qgain_ref, k_hbm, v_hbm, wo_hbm, fgain_ref, len_ref, ord_ref, part_ref,
-    pooled_ref, loss_ref, grad_ref,
+    out_ref, loss_ref,
     x_ref, qx, wq, kk, vv, wo, msg, ints, selbig, sel, bias, cosr, sinr,
     sq, qb, ob_out, ob, att, po_out, po_in, pb, st_own, st_in, ds_own, ds_in,
     pls, lb, lb_in, ub, ls_own, ls_in, uf,
-    load_sem, ss, rs, x_recv,
+    load_sem, ss, rs, x_recv, relay,
 ):
     g = lax.axis_index("dp")
     p = lax.axis_index("pack")
@@ -95,10 +95,17 @@
     def greet_pack(i):
         pl.semaphore_signal(barrier, inc=1, device_id=(g, pack_peer(i)), device_id_type=MESH)
 
-    def greet_dp(i):
-        pl.semaphore_signal(barrier, inc=1, device_id=(dp_peer(i), p), device_id_type=MESH)
-
-    each(DP - 1, greet_dp)
+    def group_at(dx, dz):
+        return lax.rem(gx + dx, 4) * 4 + lax.rem(gz + dz, 4)
+
+    near = [group_at(*d) for d in ((1, 0), (3, 0), (0, 1), (0, 3))]
+    far = [group_at(*d) for d in ((2, 0), (0, 2), (1, 1), (1, 3), (3, 1), (3, 3))]
+
+    def tell(groups, sem):
+        for to in groups:
+            pl.semaphore_signal(sem, inc=1, device_id=(to, p), device_id_type=MESH)
+
+    tell(near, barrier)
     each(PACK - 1, greet_pack)
     for load in loads:
         load.start()
@@ -123,7 +130,7 @@
         row8 == 0, sq_hi, jnp.where(row8 == 1, sq_row - sq_hi, 0.0)
     ).astype(BF16)
 
-    pl.semaphore_wait(barrier, PACK - 1 + DP - 1)
+    pl.semaphore_wait(barrier, PACK - 1 + 4)
 
     wq_copy = remote(wq_hbm.at[:, 1 - c], wq.at[c], ss.at[11], rs.at[11], g, sib)
 
@@ -137,6 +144,7 @@
 
     each(CHIPS - 1, x_start)
     wq_copy.start()
+    tell(near, relay.at[0])
     x_ref[CHIPS - 1] = msg[...]
 
     ints[...] = jnp.where(row8 == 1, -1.0, 0.0)
@@ -202,27 +210,29 @@
     wq_copy.wait_recv()
     pending.append(remote(x15, x15, ss.at[0], rs.at[0], g, sib).wait_send)
     pending.append(wq_copy.wait_send)
-    parts = [jnp.zeros((n_stmt, 128), F32), jnp.zeros((n_stmt, 128), F32)]
+    parts = jnp.zeros((n_stmt, 256), F32)
     sq_sum = jnp.zeros((8, 128), F32)
     for k in (3, 2, 1, 0):
         group = x_ref.at[4 * k:min(4 * k + 4, CHIPS - 1)]
         remote(group, group, ss.at[0], x_recv.at[k], g, sib).wait_recv()
+        if k == 0:
+            pass
         slots = list(range(4 * k, 4 * k + 4))
         blocks = jnp.concatenate([x_ref[i, 0:n_stmt, :] for i in slots], axis=1)
         for i in slots:
             sq_sum = sq_sum + x_ref[i, n_stmt:, :].astype(F32)
-        for h in range(2):
-            head = (1 - c, c)[h]
-            weights = jnp.concatenate([wq[head, source_chip(i)] for i in slots], axis=0)
-            parts[h] = parts[h] + dot(blocks, weights)
-            if k == 0 and h == 0:
-                qx[0, 0:n_stmt, :] = parts[0]
-                qx[0, n_stmt:, :] = sq_sum
-                q_copy = remote(qx.at[0], qx.at[1], ss.at[12], rs.at[12], g, sib)
-                q_copy.start()
-                pending.append(q_copy.wait_send)
+        weights = jnp.concatenate(
+            [jnp.concatenate([wq[1 - c, source_chip(i)], wq[c, source_chip(i)]], axis=1) for i in slots],
+            axis=0,
+        )
+        parts = parts + dot(blocks, weights)
+    qx[0, 0:n_stmt, :] = parts[:, 0:128]
+    qx[0, n_stmt:, :] = sq_sum
+    q_copy = remote(qx.at[0], qx.at[1], ss.at[12], rs.at[12], g, sib)
+    q_copy.start()
+    pending.append(q_copy.wait_send)
     q_copy.wait_recv()
-    q_raw = parts[1] + qx[1, 0:n_stmt, :]
+    q_raw = parts[:, 128:] + qx[1, 0:n_stmt, :]
     sq_sum = sq_sum + qx[1, n_stmt:, :]
     total = to_col(sq_sum[0:1, :] + sq_sum[1:2, :])
     mean_sq = jnp.sum(q_raw * q_raw, axis=1, keepdims=True) * (1.0 / 128.0)
@@ -239,6 +249,8 @@
     each(PACK - 1, q_start)
     qb[p] = sq[p]
     w_copy.start()
+    pl.semaphore_wait(relay.at[0], 4)
+    tell(far, relay.at[1])
     loads[1].wait()
     loads[2].wait()
     q31 = qb.at[0:PACK - 1]
@@ -304,17 +316,21 @@
     loads[3].wait()
     w_copy.wait_recv()
     remote(att.at[c], att.at[1 - c], ss.at[3], rs.at[3], g, sib).wait_recv()
+    pl.semaphore_wait(relay.at[1], 6)
     heads = jnp.concatenate([att[0], att[1]], axis=1)
-    for i in range(CHIPS):
-        to = chip_peer(i)
-        cols = pl.ds(pl.multiple_of((to * 2 + c) * 128, 128), 128)
-        w2 = jnp.concatenate([wo[0, :, cols], wo[1, :, cols]], axis=0)
-        part = dot(heads, w2)
-        if i < CHIPS - 1:
-            po_out[i] = part.astype(BF16)
-            remote(po_out.at[i], po_in.at[i], ss.at[4], rs.at[4], g, to * 2 + c).start()
-        else:
-            own_part = part
+    for k in range(CHIPS // 2):
+        ends = [chip_peer(2 * k), chip_peer(2 * k + 1)]
+        cols = [pl.ds(pl.multiple_of((to * 2 + c) * 128, 128), 128) for to in ends]
+        w4 = jnp.concatenate(
+            [jnp.concatenate([wo[0, :, at_], wo[1, :, at_]], axis=0) for at_ in cols], axis=1
+        )
+        part = dot(heads, w4)
+        for r in range(2):
+            i = 2 * k + r
+            own_part = part[:, 128 * r:128 * r + 128]
+            if i < CHIPS - 1:
+                po_out[i] = own_part.astype(BF16)
+                remote(po_out.at[i], po_in.at[i], ss.at[4], rs.at[4], g, ends[r] * 2 + c).start()
     pending.append(remote(po_out, po_in, ss.at[4], rs.at[4], g, sib).wait_send)
     remote(po_out, po_in, ss.at[4], rs.at[4], g, sib).wait_recv()
     hid = hid_ref[...].astype(F32) + own_part
@@ -368,12 +384,13 @@
     s2_all = to_col(jnp.where(lane1 < 64, pltpu.roll(st_row, 64, 1), 0.0))
     inv_norm = lax.rsqrt(s2_all)
     rms = jnp.sqrt(s1_all * (1.0 / (PACK * 128)) + EPSILON)
-    pooled_ref[...] = (hid / rms * fgain).astype(BF16)
+    out_ref[0:n_stmt, :] = (hid / rms * fgain).astype(BF16)
     remote(p15, p15, ss.at[5], rs.at[5], g, sib).wait_recv()
 
-    for j in range(8):
-        cols = pb[2 * j:2 * j + 2].reshape(128, 128)
-        pls[pl.ds(j, n_stmt, stride=8), :] = dot_t(feat, cols)
+    for j in range(4):
+        part = dot_t(feat, pb[4 * j:4 * j + 4].reshape(256, 128))
+        for r in range(2):
+            pls[pl.ds(2 * j + r, n_stmt, stride=8), :] = part[:, 128 * r:128 * r + 128]
     lb[...] = pls[...].astype(BF16).reshape(PACK, 16, 128)
 
     def l_start(i):
@@ -408,8 +425,7 @@
         target = whole(jnp.where(col_id.astype(F32) == own_partner, logit, 0.0))
         losses.append(jnp.log(whole(e)) - target)
         exps.append(e)
-    lane2 = iota((1, 2), 1)
-    loss_ref[...] = jnp.where(lane2 == 0, losses[0], losses[1])
+    loss_ref[...] = jnp.where(iota((1, 2), 1) == 0, losses[0], losses[1])
     ub[p] = jnp.concatenate(exps, axis=0).astype(BF16)
 
     def u_start(i):
@@ -453,15 +469,16 @@
     sums_all = (ls_in[0] + ls_in[1]).reshape(8, 128)
     grad = jnp.zeros((n_stmt, 128), F32)
     inner_acc = jnp.zeros((n_stmt, 128), F32)
-    for j in range(8):
-        wj = mats[j] * (inv_sum + sums_all[j:j + 1, :]) - pairs[j]
-        inner_acc = inner_acc + wj * logs[j]
-        grad = grad + dot(
-            (wj * inv_all[j:j + 1, :]).astype(BF16), pb[2 * j:2 * j + 2].reshape(128, 128)
-        )
+    for j in range(4):
+        scaled = []
+        for k in (2 * j, 2 * j + 1):
+            wk = mats[k] * (inv_sum + sums_all[k:k + 1, :]) - pairs[k]
+            inner_acc = inner_acc + wk * logs[k]
+            scaled.append((wk * inv_all[k:k + 1, :]).astype(BF16))
+        grad = grad + dot(jnp.concatenate(scaled, axis=1), pb[4 * j:4 * j + 4].reshape(256, 128))
     inner = jnp.sum(inner_acc, axis=1, keepdims=True)
     out = grad * (1.0 / WARMTH) - f32feat * (inv_norm * inner)
-    grad_ref[...] = (out * fgain * (inv_norm * float(PACK * 128) ** 0.5)).astype(BF16)
+    out_ref[n_stmt:, :] = (out * fgain * (inv_norm * float(PACK * 128) ** 0.5)).astype(BF16)
 
     for wait in pending:
         wait()
@@ -478,15 +495,14 @@
     hbm = pl.BlockSpec(memory_space=pltpu.HBM)
     V = pltpu.VMEM
     dma = pltpu.SemaphoreType.DMA
-    pooled, loss, grad = pl.pallas_call(
+    out, loss = pl.pallas_call(
         kernel,
         out_shape=(
-            jax.ShapeDtypeStruct((n, 128), BF16),
+            jax.ShapeDtypeStruct((2 * n, 128), BF16),
             jax.ShapeDtypeStruct((1, 2), F32),
-            jax.ShapeDtypeStruct((n, 128), BF16),
         ),
         in_specs=[vmem, vmem, hbm, vmem, hbm, hbm, hbm, vmem, vmem, vmem, vmem],
-        out_specs=(vmem, vmem, vmem),
+        out_specs=(vmem, vmem),
         scratch_shapes=[
             V((CHIPS, n + 8, 128), BF16),
             V((2, n + 8, 128), F32),
@@ -524,6 +540,7 @@
             dma((14,)),
             dma((14,)),
             dma((4,)),
+            pltpu.SemaphoreType.REGULAR((2,)),
         ],
         compiler_params=pltpu.CompilerParams(
             collective_id=0, has_side_effects=True
@@ -541,7 +558,7 @@
         pack_order,
         partner.reshape(8, 128),
     )
-    return pooled, loss.reshape(2), grad
+    return out[0:n], loss.reshape(2), out[n:]
 
 
 def solution(mesh):

time: 81.5 us -> 80.1 us (0.983)
  Pallas kernels: 78.2 us -> 76.6 us
    pallas_call x1, Pallas kernels: 78.2 us -> 76.6 us  [local(): pl.pallas_call(kernel, out_shape=(jax.ShapeDtypeStruct((2 * n, 128), BF16...]
    slice x0 -> x1, local copies, waits for them, and re-layouts: none -> 1.35 us  [local(): return (out[0:n], loss.reshape(2), out[n:])]
    unnamed x7 -> x3, local copies, waits for them, and re-layouts: 2.45 us -> 1.12 us
where the time goes in v3:
time: 80.1 us; the launch traced here: 79.8 us
  Pallas kernels  76.6 us (96%)
  local copies, waits for them, and re-layouts  2.47 us (3%)
    pallas_call x1, Pallas kernels, local(): pl.pallas_call(kernel, out_shape=(jax.ShapeDtypeStruct((2 * n, 128), BF16...  76.6 us

profile of v3, /device:TPU:1, one launch (start us, length us, event | category | flops | bytes accessed | tf_op | source)
XLA Modules:
  0.0 79.8 jit_solution(18215769193226161267)
XLA Ops:
  0.6 76.6 %shard_map.130 = (bf16[128,128]{1,0:T(8,128)(2,1)}, f32[1,2]{1,0:T(1,128)}) custom-call(bf16[64,128]{1,0:T(8,128)(2,1)} %hid_ref.1, f32[1,128]{1,0:T(1,128)} %bitcast.8, bf16[16,2,128,128]{3,2,1,0:T(8,128)(2,1)} %bitcast.6, f32[1,128]{1,0:T(1,128)} %bitcast.9, bf16[320,1024]{1,0:T(8,128)(2,1)} %k_hbm.1, bf16[320,1024]{1,0:T(8,128)(2,1)} %v_hbm.1, ...), custom_call_target="tpu_custom_call" | custom-call | tf_op jit(solution)/shard_map/pallas_call | solution.py:498
  77.3 1.3 %fusion = (bf16[64,128]{1,0:T(8,128)(2,1)}, bf16[64,128]{1,0:T(8,128)(2,1)}) fusion(bf16[128,128]{1,0:T(8,128)(2,1)} %get-tuple-element.5), kind=kLoop, calls=%fused_computation | loop fusion | bytes 65536 | tf_op jit(solution)/shard_map/slice | solution.py:561
  78.6 0.0 copy-start
  78.6 0.6 copy-done
  79.2 0.5 copy.15
Async XLA Ops:
  78.6 0.6 copy-start

commit v4 on v3

--- a/solution.py
+++ b/solution.py
@@ -174,28 +174,6 @@
     j3 = iota((PACK, SLOTS, 128), 1).reshape(PACK * SLOTS, 128).astype(F32)
     first_big = before(b3 * tokens)
     selbig[...] = jnp.where(place_row == first_big + j3, 1.0, 0.0).astype(BF16)
-
-    block_a = jnp.floor((start_col + 0.5) * (1.0 / tokens))
-    block_b = jnp.floor((end_col - 0.5) * (1.0 / tokens))
-    slot_a = place_col - before(block_a * tokens)
-    slot_b = place_col - before(block_b * tokens)
-    wide = iota((n_stmt, PACK * SLOTS), 1).astype(F32)
-    for i, (blk, slot) in enumerate(
-        ((block_a, slot_a), (block_b, slot_b), (block_a, float(STAT)), (block_b, float(STAT)))
-    ):
-        sel[i * n_stmt:(i + 1) * n_stmt, :] = jnp.where(
-            wide == blk * SLOTS + slot, 1.0, 0.0
-        ).astype(BF16)
-
-    pf = p.astype(F32)
-    slot_id = before(jnp.zeros((SLOTS, 128), F32) + pf * tokens) + iota((SLOTS, 1), 0).astype(F32)
-    lane24 = iota((SLOTS, 128), 1).astype(F32)
-    st = jnp.sum(jnp.where(lane24 == slot_id, start_row, 0.0), axis=1, keepdims=True)
-    en = jnp.sum(jnp.where(lane24 == slot_id, end_row, 0.0), axis=1, keepdims=True)
-    tok = iota((SLOTS, k_hbm.shape[0]), 1).astype(F32) + pf * tokens
-    own_bias = jnp.where((tok >= st) & (tok < en), 0.0, MASKED)
-    for i in range(4):
-        bias[i * SLOTS:(i + 1) * SLOTS, :] = own_bias
 
     freq = jnp.exp(
         jnp.where(lane1 < 64, lane1, lane1 - 64).astype(F32) * (-2.0 / 128.0 * math.log(ROPE_BASE))
@@ -240,15 +218,40 @@
     q = q_raw * inv * qgain_ref[...]
     q = (q * cosr[...] + pltpu.roll(q, 64, 1) * sinr[...]).astype(BF16)
     q128 = jnp.concatenate([q, jnp.zeros((128 - n_stmt, 128), BF16)], axis=0)
-    sq[...] = dot(selbig[...], q128).astype(BF16).reshape(PACK, SLOTS, 128)
-
-    def q_start(i):
-        to = pack_peer(i)
-        remote(sq.at[to], qb.at[p], ss.at[1], rs.at[1], g, to).start()
-
-    each(PACK - 1, q_start)
+    for k in range(8):
+        py = lax.rem(y + far_first(k, 4), 8)
+        firsts = [py * 2, py * 2 + 16]
+        rows = [pl.ds(pl.multiple_of(f * SLOTS, 16), 2 * SLOTS) for f in firsts]
+        chosen = dot(jnp.concatenate([selbig[r, :] for r in rows], axis=0), q128).astype(BF16)
+        for f, r in zip(firsts, (0, 1)):
+            sq[pl.ds(f, 2)] = chosen[2 * SLOTS * r:2 * SLOTS * (r + 1)].reshape(2, SLOTS, 128)
+        for i in range(4 * k, min(4 * k + 4, PACK - 1)):
+            to = pack_peer(i)
+            remote(sq.at[to], qb.at[p], ss.at[1], rs.at[1], g, to).start()
     qb[p] = sq[p]
     w_copy.start()
+    block_a = jnp.floor((start_col + 0.5) * (1.0 / tokens))
+    block_b = jnp.floor((end_col - 0.5) * (1.0 / tokens))
+    slot_a = place_col - before(block_a * tokens)
+    slot_b = place_col - before(block_b * tokens)
+    wide = iota((n_stmt, PACK * SLOTS), 1).astype(F32)
+    for i, (blk, slot) in enumerate(
+        ((block_a, slot_a), (block_b, slot_b), (block_a, float(STAT)), (block_b, float(STAT)))
+    ):
+        sel[i * n_stmt:(i + 1) * n_stmt, :] = jnp.where(
+            wide == blk * SLOTS + slot, 1.0, 0.0
+        ).astype(BF16)
+
+    pf = p.astype(F32)
+    slot_id = before(jnp.zeros((SLOTS, 128), F32) + pf * tokens) + iota((SLOTS, 1), 0).astype(F32)
+    lane24 = iota((SLOTS, 128), 1).astype(F32)
+    st = jnp.sum(jnp.where(lane24 == slot_id, start_row, 0.0), axis=1, keepdims=True)
+    en = jnp.sum(jnp.where(lane24 == slot_id, end_row, 0.0), axis=1, keepdims=True)
+    tok = iota((SLOTS, k_hbm.shape[0]), 1).astype(F32) + pf * tokens
+    own_bias = jnp.where((tok >= st) & (tok < en), 0.0, MASKED)
+    for i in range(4):
+        bias[i * SLOTS:(i + 1) * SLOTS, :] = own_bias
+
     pl.semaphore_wait(relay.at[0], 4)
     tell(far, relay.at[1])
     loads[1].wait()

time: 80.1 us -> 80.5 us (level)
  no operation moved by 1% of the time
where the time goes in v4:
time: 80.5 us; the launch traced here: 80.1 us
  Pallas kernels  77 us (96%)
  local copies, waits for them, and re-layouts  2.47 us (3%)
    pallas_call x1, Pallas kernels, local(): pl.pallas_call(kernel, out_shape=(jax.ShapeDtypeStruct((2 * n, 128), BF16...  77 us

profile of v4, /device:TPU:1, one launch (start us, length us, event | category | flops | bytes accessed | tf_op | source)
XLA Modules:
  0.0 80.1 jit_solution(6705519990997193813)
XLA Ops:
  0.6 77.0 %shard_map.130 = (bf16[128,128]{1,0:T(8,128)(2,1)}, f32[1,2]{1,0:T(1,128)}) custom-call(bf16[64,128]{1,0:T(8,128)(2,1)} %hid_ref.1, f32[1,128]{1,0:T(1,128)} %bitcast.8, bf16[16,2,128,128]{3,2,1,0:T(8,128)(2,1)} %bitcast.6, f32[1,128]{1,0:T(1,128)} %bitcast.9, bf16[320,1024]{1,0:T(8,128)(2,1)} %k_hbm.1, bf16[320,1024]{1,0:T(8,128)(2,1)} %v_hbm.1, ...), custom_call_target="tpu_custom_call" | custom-call | tf_op jit(solution)/shard_map/pallas_call | solution.py:501
  77.6 1.3 %fusion = (bf16[64,128]{1,0:T(8,128)(2,1)}, bf16[64,128]{1,0:T(8,128)(2,1)}) fusion(bf16[128,128]{1,0:T(8,128)(2,1)} %get-tuple-element.5), kind=kLoop, calls=%fused_computation | loop fusion | bytes 65536 | tf_op jit(solution)/shard_map/slice | solution.py:564
  79.0 0.0 copy-start
  79.0 0.6 copy-done
  79.6 0.5 copy.15
Async XLA Ops:
  79.0 0.6 copy-start

commit v5 on v4

--- a/solution.py
+++ b/solution.py
@@ -49,7 +49,7 @@
     out_ref, loss_ref,
     x_ref, qx, wq, kk, vv, wo, msg, ints, selbig, sel, bias, cosr, sinr,
     sq, qb, ob_out, ob, att, po_out, po_in, pb, st_own, st_in, ds_own, ds_in,
-    pls, lb, lb_in, ub, ls_own, ls_in, uf,
+    pls, lb, lb_in, ub, ls_own, ls_in, uf, a_own, a_in,
     load_sem, ss, rs, x_recv, relay,
 ):
     g = lax.axis_index("dp")
@@ -418,6 +418,7 @@
 
     losses = []
     exps = []
+    sums = []
     for i in range(2):
         row_id = g * n_stmt + p * 2 + i
         diag = col_id == row_id
@@ -426,9 +427,18 @@
         e = jnp.where(diag, 0.0, jnp.exp(logit))
         own_partner = whole(jnp.where(diag, partner.astype(F32), 0.0))
         target = whole(jnp.where(col_id.astype(F32) == own_partner, logit, 0.0))
-        losses.append(jnp.log(whole(e)) - target)
+        sums.append(whole(e))
+        losses.append(jnp.log(sums[i]) - target)
         exps.append(e)
     loss_ref[...] = jnp.where(iota((1, 2), 1) == 0, losses[0], losses[1])
+    first = lane1 - 64 * odd
+    ls_own[...] = jnp.where(first == 0, 1.0 / sums[0], jnp.where(first == 1, 1.0 / sums[1], 0.0))
+    ls_in[odd, half_row] = ls_own[...]
+
+    def e_start(i):
+        remote(ls_own, ls_in.at[odd, half_row], ss.at[10], rs.at[10], dp_peer(i), p).start()
+
+    each(DP - 1, e_start)
     ub[p] = jnp.concatenate(exps, axis=0).astype(BF16)
 
     def u_start(i):
@@ -437,21 +447,6 @@
     each(PACK - 1, u_start)
     u31 = ub.at[0:PACK - 1]
     pending.append(remote(u31, u31, ss.at[9], rs.at[9], g, sib).wait_send)
-    remote(u31, u31, ss.at[9], rs.at[9], g, sib).wait_recv()
-    uf[...] = ub[...].reshape(PACK * 16, 128).astype(F32)
-    mats = [uf[pl.ds(j, n_stmt, stride=8), :] for j in range(8)]
-    row_sum = mats[0]
-    for j in range(1, 8):
-        row_sum = row_sum + mats[j]
-    inv_sum = 1.0 / jnp.sum(row_sum, axis=1, keepdims=True)
-    inv_row = jnp.sum(jnp.where(lane == sub + 64, inv_sum, 0.0), axis=0, keepdims=True)
-    ls_own[...] = own_half(inv_row)
-    ls_in[odd, half_row] = ls_own[...]
-
-    def e_start(i):
-        remote(ls_own, ls_in.at[odd, half_row], ss.at[10], rs.at[10], dp_peer(i), p).start()
-
-    each(DP - 1, e_start)
     row_f = (g * n_stmt + iota((n_stmt, 1), 0)).astype(F32)
     part_f = partner.astype(F32)
     own_part_col = jnp.zeros((n_stmt, 1), F32)
@@ -460,22 +455,54 @@
             jnp.where((lane + 128 * j).astype(F32) == row_f, part_f[j:j + 1, :], 0.0), axis=1, keepdims=True
         )
     pairs = []
-    logs = []
     for j in range(8):
         cid = (lane + 128 * j).astype(F32)
         pairs.append(
             jnp.where(cid == own_part_col, 1.0, 0.0) + jnp.where(part_f[j:j + 1, :] == row_f, 1.0, 0.0)
         )
-        logs.append(jnp.log(jnp.maximum(mats[j], 1e-30)))
     pending.append(remote(dall, dall, ss.at[10], rs.at[10], g, sib).wait_send)
     remote(dall, dall, ss.at[10], rs.at[10], g, sib).wait_recv()
-    sums_all = (ls_in[0] + ls_in[1]).reshape(8, 128)
+    mine = (ls_in[0] + ls_in[1]).reshape(8, 128)
+    packed = mine[0:1, :]
+    for j in range(1, 8):
+        packed = packed + pltpu.roll(mine[j:j + 1, :], 2 * j, 1)
+    a_own[...] = packed
+    a_in[p] = packed
+
+    def a_start(i):
+        remote(a_own, a_in.at[p], ss.at[14], rs.at[14], g, pack_peer(i)).start()
+
+    each(PACK - 1, a_start)
+    a31 = a_in.at[0:PACK - 1]
+    pending.append(remote(a31, a31, ss.at[14], rs.at[14], g, sib).wait_send)
+    remote(u31, u31, ss.at[9], rs.at[9], g, sib).wait_recv()
+    uf[...] = ub[...].reshape(PACK * 16, 128).astype(F32)
+    mats = [uf[pl.ds(j, n_stmt, stride=8), :] for j in range(8)]
+    row_sum = mats[0]
+    for j in range(1, 8):
+        row_sum = row_sum + mats[j]
+    inv_sum = 1.0 / jnp.sum(row_sum, axis=1, keepdims=True)
+    logs = [jnp.log(jnp.maximum(m, 1e-30)) for m in mats]
+    remote(a31, a31, ss.at[14], rs.at[14], g, sib).wait_recv()
+    arrived = a_in[...].reshape(PACK, 128)
+    lane32 = iota((PACK, 128), 1)
+    place = lax.rem(lane32, 64)
+    here = lax.div(place, 2) == iota((PACK, 128), 0)
+    second = lax.rem(place, 2) == 1
+    upper = lane32 >= 64
+    sums_all = []
+    for j in range(8):
+        low = jnp.where(second, arrived[:, 2 * j + 1:2 * j + 2], arrived[:, 2 * j:2 * j + 1])
+        high = jnp.where(second, arrived[:, 64 + 2 * j + 1:64 + 2 * j + 2], arrived[:, 64 + 2 * j:64 + 2 * j + 1])
+        sums_all.append(
+            jnp.sum(jnp.where(here, jnp.where(upper, high, low), 0.0), axis=0, keepdims=True)
+        )
     grad = jnp.zeros((n_stmt, 128), F32)
     inner_acc = jnp.zeros((n_stmt, 128), F32)
     for j in range(4):
         scaled = []
         for k in (2 * j, 2 * j + 1):
-            wk = mats[k] * (inv_sum + sums_all[k:k + 1, :]) - pairs[k]
+            wk = mats[k] * (inv_sum + sums_all[k]) - pairs[k]
             inner_acc = inner_acc + wk * logs[k]
             scaled.append((wk * inv_all[k:k + 1, :]).astype(BF16))
         grad = grad + dot(jnp.concatenate(scaled, axis=1), pb[4 * j:4 * j + 4].reshape(256, 128))
@@ -539,9 +566,11 @@
             V((1, 128), F32),
             V((2, 8, 1, 128), F32),
             V((n * 8, 128), F32),
+            V((1, 128), F32),
+            V((PACK, 1, 128), F32),
             dma((4,)),
-            dma((14,)),
-            dma((14,)),
+            dma((15,)),
+            dma((15,)),
             dma((4,)),
             pltpu.SemaphoreType.REGULAR((2,)),
         ],

time: 80.5 us -> 81.6 us (1.014)
  Pallas kernels: 77 us -> 78.1 us
    pallas_call x1, Pallas kernels: 77 us -> 78.1 us  [local(): pl.pallas_call(kernel, out_shape=(jax.ShapeDtypeStruct((2 * n, 128), BF16...]
where the time goes in v5:
time: 81.6 us; the launch traced here: 81.2 us
  Pallas kernels  78.1 us (96%)
  local copies, waits for them, and re-layouts  2.47 us (3%)
    pallas_call x1, Pallas kernels, local(): pl.pallas_call(kernel, out_shape=(jax.ShapeDtypeStruct((2 * n, 128), BF16...  78.1 us

profile of v5, /device:TPU:1, one launch (start us, length us, event | category | flops | bytes accessed | tf_op | source)
XLA Modules:
  0.0 81.2 jit_solution(11088656115360128217)
XLA Ops:
  0.6 78.1 %shard_map.130 = (bf16[128,128]{1,0:T(8,128)(2,1)}, f32[1,2]{1,0:T(1,128)}) custom-call(bf16[64,128]{1,0:T(8,128)(2,1)} %hid_ref.1, f32[1,128]{1,0:T(1,128)} %bitcast.8, bf16[16,2,128,128]{3,2,1,0:T(8,128)(2,1)} %bitcast.6, f32[1,128]{1,0:T(1,128)} %bitcast.9, bf16[320,1024]{1,0:T(8,128)(2,1)} %k_hbm.1, bf16[320,1024]{1,0:T(8,128)(2,1)} %v_hbm.1, ...), custom_call_target="tpu_custom_call" | custom-call | tf_op jit(solution)/shard_map/pallas_call | solution.py:528
  78.8 1.3 %fusion = (bf16[64,128]{1,0:T(8,128)(2,1)}, bf16[64,128]{1,0:T(8,128)(2,1)}) fusion(bf16[128,128]{1,0:T(8,128)(2,1)} %get-tuple-element.5), kind=kLoop, calls=%fused_computation | loop fusion | bytes 65536 | tf_op jit(solution)/shard_map/slice | solution.py:593
  80.1 0.0 copy-start
  80.1 0.6 copy-done
  80.7 0.5 copy.15
Async XLA Ops:
  80.1 0.6 copy-start

commit v6 on v4

--- a/solution.py
+++ b/solution.py
@@ -45,9 +45,9 @@
 
 
 def kernel(
-    hid_ref, again_ref, wq_hbm, qgain_ref, k_hbm, v_hbm, wo_hbm, fgain_ref, len_ref, ord_ref, part_ref,
+    hid_hbm, again_hbm, wq_hbm, qgain_hbm, k_hbm, v_hbm, wo_hbm, fgain_hbm, len_hbm, ord_hbm, part_hbm,
     out_ref, loss_ref,
-    x_ref, qx, wq, kk, vv, wo, msg, ints, selbig, sel, bias, cosr, sinr,
+    hid_ref, again_ref, qgain_ref, fgain_ref, len_ref, ord_ref, part_ref, x_ref, qx, wq, kk, vv, wo, msg, ints, selbig, sel, bias, cosr, sinr,
     sq, qb, ob_out, ob, att, po_out, po_in, pb, st_own, st_in, ds_own, ds_in,
     pls, lb, lb_in, ub, ls_own, ls_in, uf,
     load_sem, ss, rs, x_recv, relay,
@@ -57,7 +57,7 @@
     z, y, c = lax.div(p, 16), lax.div(lax.rem(p, 16), 2), lax.rem(p, 2)
     sib = p + 1 - 2 * c
     chip = z * 8 + y
-    n_stmt = hid_ref.shape[0]
+    n_stmt = hid_hbm.shape[0]
 
     def pack_peer(i):
         k, r = i // 4, i % 4
@@ -90,6 +90,15 @@
         pltpu.make_async_copy(v_hbm, vv, load_sem.at[2]),
         pltpu.make_async_copy(wo_hbm, wo.at[c], load_sem.at[3]),
     ]
+    small = [
+        pltpu.make_async_copy(src, dst, load_sem.at[4 + i])
+        for i, (src, dst) in enumerate((
+            (hid_hbm, hid_ref), (again_hbm, again_ref), (len_hbm, len_ref), (ord_hbm, ord_ref),
+            (qgain_hbm, qgain_ref), (fgain_hbm, fgain_ref), (part_hbm, part_ref),
+        ))
+    ]
+    small[0].start()
+    small[1].start()
     barrier = pltpu.get_barrier_semaphore()
 
     def greet_pack(i):
@@ -107,7 +116,7 @@
 
     tell(near, barrier)
     each(PACK - 1, greet_pack)
-    for load in loads:
+    for load in small[2:] + loads:
         load.start()
 
     lane = iota((n_stmt, 128), 1)
@@ -122,6 +131,8 @@
         return jnp.sum(jnp.where(same, row, 0.0), axis=1, keepdims=True)
 
     row8 = iota((8, 128), 0)
+    small[0].wait()
+    small[1].wait()
     h32 = hid_ref[...].astype(F32)
     msg[0:n_stmt, :] = (h32 * again_ref[...]).astype(BF16)
     sq_row = to_row(jnp.sum(h32 * h32, axis=1, keepdims=True))
@@ -147,6 +158,8 @@
     tell(near, relay.at[0])
     x_ref[CHIPS - 1] = msg[...]
 
+    for load in small[2:]:
+        load.wait()
     ints[...] = jnp.where(row8 == 1, -1.0, 0.0)
     ints[0:1, 0:n_stmt] = len_ref[...].astype(F32)
     ints[1:2, 0:n_stmt] = ord_ref[...].astype(F32)
@@ -504,9 +517,16 @@
             jax.ShapeDtypeStruct((2 * n, 128), BF16),
             jax.ShapeDtypeStruct((1, 2), F32),
         ),
-        in_specs=[vmem, vmem, hbm, vmem, hbm, hbm, hbm, vmem, vmem, vmem, vmem],
+        in_specs=[hbm] * 11,
         out_specs=(vmem, vmem),
         scratch_shapes=[
+            V((n, 128), BF16),
+            V((1, 128), F32),
+            V((1, 128), F32),
+            V((1, 128), F32),
+            V(lengths.shape, I32),
+            V(pack_order.shape, I32),
+            V((8, 128), I32),
             V((CHIPS, n + 8, 128), BF16),
             V((2, n + 8, 128), F32),
             V((2, CHIPS, 128, 128), BF16),
@@ -539,7 +559,7 @@
             V((1, 128), F32),
             V((2, 8, 1, 128), F32),
             V((n * 8, 128), F32),
-            dma((4,)),
+            dma((11,)),
             dma((14,)),
             dma((14,)),
             dma((4,)),

time: 80.5 us -> 80 us (level)
  no operation moved by 1% of the time
where the time goes in v6:
time: 80 us; the launch traced here: 79.5 us
  Pallas kernels  76.4 us (96%)
  local copies, waits for them, and re-layouts  2.47 us (3%)
    pallas_call x1, Pallas kernels, local(): pl.pallas_call(kernel, out_shape=(jax.ShapeDtypeStruct((2 * n, 128), BF16...  76.4 us

profile of v6, /device:TPU:1, one launch (start us, length us, event | category | flops | bytes accessed | tf_op | source)
XLA Modules:
  0.0 79.5 jit_solution(13998536956896810646)
XLA Ops:
  0.6 76.4 %shard_map.130 = (bf16[128,128]{1,0:T(8,128)(2,1)}, f32[1,2]{1,0:T(1,128)}) custom-call(bf16[64,128]{1,0:T(8,128)(2,1)} %hid_hbm.1, f32[1,128]{1,0:T(1,128)} %bitcast.8, bf16[16,2,128,128]{3,2,1,0:T(8,128)(2,1)} %bitcast.6, f32[1,128]{1,0:T(1,128)} %bitcast.9, bf16[320,1024]{1,0:T(8,128)(2,1)} %k_hbm.1, bf16[320,1024]{1,0:T(8,128)(2,1)} %v_hbm.1, ...), custom_call_target="tpu_custom_call" | custom-call | tf_op jit(solution)/shard_map/pallas_call | solution.py:514
  77.1 1.3 %fusion = (bf16[64,128]{1,0:T(8,128)(2,1)}, bf16[64,128]{1,0:T(8,128)(2,1)}) fusion(bf16[128,128]{1,0:T(8,128)(2,1)} %get-tuple-element.5), kind=kLoop, calls=%fused_computation | loop fusion | bytes 65536 | tf_op jit(solution)/shard_map/slice | solution.py:584
  78.4 0.0 copy-start
  78.4 0.6 copy-done
  79.0 0.5 copy.15
Async XLA Ops:
  78.4 0.6 copy-start

commit v7 on v6

--- a/solution.py
+++ b/solution.py
@@ -441,7 +441,7 @@
         target = whole(jnp.where(col_id.astype(F32) == own_partner, logit, 0.0))
         losses.append(jnp.log(whole(e)) - target)
         exps.append(e)
-    loss_ref[...] = jnp.where(iota((1, 2), 1) == 0, losses[0], losses[1])
+    loss_ref[...] = jnp.where(iota((8, 128), 1) == 0, losses[0], losses[1])
     ub[p] = jnp.concatenate(exps, axis=0).astype(BF16)
 
     def u_start(i):
@@ -515,7 +515,7 @@
         kernel,
         out_shape=(
             jax.ShapeDtypeStruct((2 * n, 128), BF16),
-            jax.ShapeDtypeStruct((1, 2), F32),
+            jax.ShapeDtypeStruct((8, 128), F32),
         ),
         in_specs=[hbm] * 11,
         out_specs=(vmem, vmem),
@@ -581,7 +581,7 @@
         pack_order,
         partner.reshape(8, 128),
     )
-    return out[0:n], loss.reshape(2), out[n:]
+    return out[0:n], loss[0, 0:2], out[n:]
 
 
 def solution(mesh):

time: 80 us -> 80 us (level)
    squeeze x0 -> x1, local copies, waits for them, and re-layouts: none -> 1.18 us  [local(): return (out[0:n], loss[0, 0:2], out[n:])]
    unnamed x3 -> x0, local copies, waits for them, and re-layouts: 1.12 us -> none
where the time goes in v7:
time: 80 us; the launch traced here: 79.6 us
  Pallas kernels  76.4 us (96%)
  local copies, waits for them, and re-layouts  2.53 us (3%)
    pallas_call x1, Pallas kernels, local(): pl.pallas_call(kernel, out_shape=(jax.ShapeDtypeStruct((2 * n, 128), BF16...  76.4 us

profile of v7, /device:TPU:1, one launch (start us, length us, event | category | flops | bytes accessed | tf_op | source)
XLA Modules:
  0.0 79.6 jit_solution(14862398608428547938)
XLA Ops:
  0.6 76.4 %shard_map.130 = (bf16[128,128]{1,0:T(8,128)(2,1)}, f32[8,128]{1,0:T(8,128)}) custom-call(bf16[64,128]{1,0:T(8,128)(2,1)} %hid_hbm.1, f32[1,128]{1,0:T(1,128)} %bitcast.9, bf16[16,2,128,128]{3,2,1,0:T(8,128)(2,1)} %bitcast.7, f32[1,128]{1,0:T(1,128)} %bitcast.10, bf16[320,1024]{1,0:T(8,128)(2,1)} %k_hbm.1, bf16[320,1024]{1,0:T(8,128)(2,1)} %v_hbm.1, ...), custom_call_target="tpu_custom_call" | custom-call | tf_op jit(solution)/shard_map/pallas_call | solution.py:514
  77.1 1.3 %fusion = (bf16[64,128]{1,0:T(8,128)(2,1)}, bf16[64,128]{1,0:T(8,128)(2,1)}) fusion(bf16[128,128]{1,0:T(8,128)(2,1)} %get-tuple-element.5), kind=kLoop, calls=%fused_computation.1 | loop fusion | bytes 65536 | tf_op jit(solution)/shard_map/slice | solution.py:584
  78.4 1.2 %slice_bitcast_fusion = f32[2]{0:T(128)} fusion(f32[8,128]{1,0:T(8,128)} %get-tuple-element.6), kind=kLoop, calls=%fused_computation | loop fusion | bytes 16 | tf_op jit(solution)/shard_map/squeeze | solution.py:584
